TPU v7x, 32 devices: a whole 2x2x4 slice. The times are simulated.
32 devices in a mesh: groups: 2 (over x), streams: 16 (over z, y, core).
Axes of the slice: x: 2, y: 2, z: 4, core: 2. Of those that a mesh axis runs over, the one named last changes fastest.
Arguments:
- frames: bfloat16 [4096, 1536], P(('groups', 'streams')), parts along dimension 0, may hold values from -500 to 500
- route_peer: int32 [4096], P(('groups', 'streams')), parts along dimension 0, may hold values from 0 to 15, as said below
- route_pos: int32 [4096], P(('groups', 'streams')), parts along dimension 0, may hold values from 0 to 127
- destination: int32 [256], P(('groups', 'streams')), parts along dimension 0, may hold values from 0 to 127, as said below
- valid_count: int32 [256], P(('groups', 'streams')), parts along dimension 0, may hold values from 1 to 16
- key_cache: bfloat16 [256, 32, 768], P(('groups', 'streams')), parts along dimension 0, may hold values from -700 to 700
- value_cache: bfloat16 [256, 32, 768], P(('groups', 'streams')), parts along dimension 0, may hold values from -4 to 4
- conv_state: bfloat16 [256, 31, 768], P(('groups', 'streams')), parts along dimension 0, may hold values from -4 to 4
- qkv_weight: bfloat16 [1536, 2304], replicated, may hold values from -0.15625 to 0.15625
- conv_kernel: bfloat16 [32, 768], replicated, may hold values from -1 to 1
Outputs:
- encoded: bfloat16 [4096, 768], P(('groups', 'streams')), parts along dimension 0
- keys_next: bfloat16 [256, 32, 768], P(('groups', 'streams')), parts along dimension 0
- values_next: bfloat16 [256, 32, 768], P(('groups', 'streams')), parts along dimension 0
- conv_next: bfloat16 [256, 31, 768], P(('groups', 'streams')), parts along dimension 0
There are 2 independent parts, one for each index of `groups`. A program takes and returns all parts, laid end to end along the dimension named above; an argument that names none is the same for every part. Nothing has to cross between parts.
Inputs may be any that keep to these rules, and one draw needn't show every extreme that they name: `route_peer`: each owner slot of a part receives exactly one frame row; the rows one ingest device sends to one owner number at most 12, and exactly 12 to some owner in every draw. `destination`: A permutation of the 128 slots. A stream stays on its device or moves to the device one index up or down along streams, wrapping; at most 4 streams go from one device to each neighbour, and exactly 4 from some device in every draw.
All inputs are finite; a program needn't handle non-finite values.
Results may differ from a plain program's by a relative error of at most 0.0059.
Values may be sent and summed in bfloat16 or wider, within the bound.
No kernel may reach another device: no remote copies, remote signals or barrier semaphores. Data moves between devices by JAX's collectives and lax.ppermute only.
A program may use at most 64 MiB of HBM per device.

v0:
```python
import jax
import jax.numpy as jnp
from jax import lax
from jax.sharding import PartitionSpec as P

HEAD = 96
MIG = 4


EPSILON = 1e-05


def from_behind(block, axis, distance):
    devices = range(lax.axis_size(axis))
    route = [((i - distance) % len(devices), i) for i in devices]
    return lax.ppermute(block, axis, route)


def layer_norm(matrix):
    widened = matrix.astype(jnp.float32)
    centered = widened - jnp.mean(widened, axis=-1, keepdims=True)
    spread = jnp.mean(centered * centered, axis=-1, keepdims=True)
    return (centered * lax.rsqrt(spread + EPSILON)).astype(jnp.bfloat16)


def project(payload, qkv_weight):
    return jnp.einsum(
        "...d,de->...e", layer_norm(payload), qkv_weight, preferred_element_type=jnp.float32
    ).astype(jnp.bfloat16)


def select_rows(selector, source):
    return jnp.einsum("sij,sjc->sic", selector, source, preferred_element_type=jnp.float32).astype(
        source.dtype
    )


def stream_step(qkv_rows, old_keys, old_values, old_conv, valid_count, conv_kernel):
    streams_here, span_len, triple = qkv_rows.shape
    qkv_width = triple // 3
    head_count = qkv_width // HEAD
    left_len = old_keys.shape[1]
    key_len = left_len + span_len
    keys_all = jnp.concatenate([old_keys, qkv_rows[:, :, qkv_width : 2 * qkv_width]], axis=1)
    values_all = jnp.concatenate([old_values, qkv_rows[:, :, 2 * qkv_width :]], axis=1)
    query_heads = qkv_rows[:, :, :qkv_width].reshape(streams_here, span_len, head_count, HEAD)
    key_heads = keys_all.reshape(streams_here, key_len, head_count, HEAD)
    value_heads = values_all.reshape(streams_here, key_len, head_count, HEAD)
    scores = jnp.einsum(
        "sqhd,skhd->shqk", query_heads, key_heads, preferred_element_type=jnp.float32
    ) * HEAD ** (-0.5)
    query_pos = jnp.arange(span_len, dtype=jnp.int32)[:, None]
    key_pos = jnp.arange(key_len, dtype=jnp.int32)[None, :] - left_len
    causal = (key_pos <= query_pos)[None]
    filled = key_pos[None] < valid_count[:, None, None]
    allowed = (key_pos[None] < 0) | causal & filled
    scores = jnp.where(allowed[:, None], scores, -1e30)
    row_max = jnp.max(scores, axis=-1, keepdims=True)
    weights_exp = jnp.exp(scores - row_max)
    probabilities = (weights_exp / jnp.sum(weights_exp, axis=-1, keepdims=True)).astype(
        jnp.bfloat16
    )
    mixed_heads = jnp.einsum(
        "shqk,skhd->sqhd", probabilities, value_heads, preferred_element_type=jnp.float32
    )
    alive_rows = jnp.arange(span_len, dtype=jnp.int32)[None, :] < valid_count[:, None]
    attended = jnp.where(alive_rows[:, :, None, None], mixed_heads, 0.0)
    attended = attended.reshape(streams_here, span_len, qkv_width).astype(jnp.bfloat16)
    attended = lax.optimization_barrier(attended)
    conv_input = jnp.concatenate([old_conv, attended], axis=1)
    kernel_len = conv_kernel.shape[0]
    summed = attended.astype(jnp.float32)
    for offset_tap in range(kernel_len):
        window = conv_input[:, offset_tap : offset_tap + span_len].astype(jnp.float32)
        summed = summed + conv_kernel[offset_tap].astype(jnp.float32) * window
    encoded = jnp.where(alive_rows[:, :, None], summed, 0.0).astype(jnp.bfloat16)
    key_want = valid_count[:, None, None] + jnp.arange(left_len, dtype=jnp.int32)[None, :, None]
    key_select = (key_want == jnp.arange(key_len, dtype=jnp.int32)[None, None, :]).astype(
        jnp.bfloat16
    )
    keys_next = select_rows(key_select, keys_all)
    values_next = select_rows(key_select, values_all)
    conv_len = kernel_len - 1 + span_len
    conv_want = (
        valid_count[:, None, None] + jnp.arange(kernel_len - 1, dtype=jnp.int32)[None, :, None]
    )
    conv_select = (conv_want == jnp.arange(conv_len, dtype=jnp.int32)[None, None, :]).astype(
        jnp.bfloat16
    )
    conv_next = select_rows(conv_select, conv_input)
    return (encoded.reshape(streams_here * span_len, qkv_width), keys_next, values_next, conv_next)


def local(
    frames,
    route_peer,
    route_pos,
    destination,
    valid_count,
    key_cache,
    value_cache,
    conv_state,
    qkv_weight,
    conv_kernel,
):
    peer_count = lax.axis_size("streams")
    row_count = frames.shape[0]
    per_peer = row_count // peer_count
    capacity = per_peer + per_peer // 2
    streams_here = key_cache.shape[0]
    span_len = row_count // streams_here
    peer_ids = jnp.arange(peer_count, dtype=jnp.int32)
    one_hot = (route_peer[:, None] == peer_ids[None, :]).astype(jnp.int32)
    running = jnp.cumsum(one_hot, axis=0) - 1
    slot_index = jnp.sum(running * one_hot, axis=1)
    flat_slot = route_peer * capacity + slot_index
    send_ints = (
        jnp.arange(peer_count * capacity, dtype=jnp.int32)[:, None] == flat_slot[None, :]
    ).astype(jnp.int32)
    send_matrix = send_ints.astype(jnp.bfloat16)
    filled_slot = jnp.sum(send_ints, axis=1)
    where_flat = jnp.sum(send_ints * route_pos[None, :], axis=1) + row_count * (1 - filled_slot)
    where_to = where_flat.reshape(peer_count, capacity)
    packed = jnp.dot(send_matrix, frames, preferred_element_type=jnp.float32).astype(frames.dtype)
    outgoing = packed.reshape(peer_count, capacity, frames.shape[1])
    received = project(
        lax.all_to_all(outgoing, "streams", split_axis=0, concat_axis=0, tiled=True), qkv_weight
    )
    positions = lax.all_to_all(where_to, "streams", split_axis=0, concat_axis=0, tiled=True)
    flattened = received.reshape(-1, received.shape[-1])
    placing = (
        jnp.arange(row_count, dtype=jnp.int32)[:, None] == positions.reshape(-1)[None, :]
    ).astype(received.dtype)
    qkv_rows = jnp.dot(placing, flattened, preferred_element_type=jnp.float32).astype(
        received.dtype
    )
    own_index = lax.axis_index("streams")
    target_device = destination // streams_here
    target_slot = destination % streams_here
    upper_device = (own_index + 1) % peer_count
    lower_device = (own_index + peer_count - 1) % peer_count
    staying = target_device == own_index
    slot_range = jnp.arange(streams_here, dtype=jnp.int32)

    def apply_rows(selector, state_block):
        flat_state = state_block.reshape(state_block.shape[0], -1)
        result = jnp.dot(selector, flat_state, preferred_element_type=jnp.float32)
        return result.reshape((selector.shape[0],) + state_block.shape[1:])

    def bundle(chosen):
        ranking = jnp.cumsum(chosen.astype(jnp.int32)) - 1
        slot_pick = jnp.where(chosen, ranking, MIG)
        pick_ints = (jnp.arange(MIG, dtype=jnp.int32)[:, None] == slot_pick[None, :]).astype(
            jnp.int32
        )
        picker = pick_ints.astype(jnp.bfloat16)
        slot_list = jnp.sum(pick_ints * target_slot[None, :], axis=1) + streams_here * (
            1 - jnp.sum(pick_ints, axis=1)
        )
        return (
            apply_rows(picker, key_cache).astype(jnp.bfloat16),
            apply_rows(picker, value_cache).astype(jnp.bfloat16),
            apply_rows(picker, conv_state).astype(jnp.bfloat16),
            slot_list,
        )

    up_keys, up_values, up_conv, up_slots = bundle(target_device == upper_device)
    from_lower = from_behind((up_keys, up_values, up_conv, up_slots), "streams", 1)
    down_keys, down_values, down_conv, down_slots = bundle(target_device == lower_device)
    from_upper = from_behind((down_keys, down_values, down_conv, down_slots), "streams", -1)
    home_slot = jnp.where(staying, target_slot, streams_here)
    home_matrix = (slot_range[:, None] == home_slot[None, :]).astype(jnp.bfloat16)
    lower_matrix = (slot_range[:, None] == from_lower[3][None, :]).astype(jnp.bfloat16)
    upper_matrix = (slot_range[:, None] == from_upper[3][None, :]).astype(jnp.bfloat16)

    def settle(previous, member):
        rebuilt = apply_rows(home_matrix, previous)
        rebuilt = rebuilt + apply_rows(lower_matrix, from_lower[member])
        rebuilt = rebuilt + apply_rows(upper_matrix, from_upper[member])
        return rebuilt.astype(previous.dtype)

    moved_keys = settle(key_cache, 0)
    moved_values = settle(value_cache, 1)
    moved_conv = settle(conv_state, 2)
    encoded, keys_next, values_next, conv_next = stream_step(
        qkv_rows.reshape(streams_here, span_len, -1),
        moved_keys,
        moved_values,
        moved_conv,
        valid_count,
        conv_kernel,
    )
    return (encoded, keys_next, values_next, conv_next)


def solution(mesh):
    return jax.shard_map(
        local,
        mesh=mesh,
        in_specs=(
            P(("groups", "streams"), None),
            P(("groups", "streams")),
            P(("groups", "streams")),
            P(("groups", "streams")),
            P(("groups", "streams")),
            P(("groups", "streams"), None, None),
            P(("groups", "streams"), None, None),
            P(("groups", "streams"), None, None),
            P(),
            P(),
        ),
        out_specs=(
            P(("groups", "streams"), None),
            P(("groups", "streams"), None, None),
            P(("groups", "streams"), None, None),
            P(("groups", "streams"), None, None),
        ),
        check_vma=False,
    )
```

profile of v0, /device:TPU:15, one launch (start us, length us, event | category | flops | bytes accessed | tf_op | source)
XLA Modules:
  0.0 87.8 jit_solution(16902912872685744388)
XLA Ops:
  3.2 1.8 %collective-permute-start = (s32[4]{0:T(128)}, s32[4]{0:T(128)}, u32[]{:S(2)}, u32[]{:S(2)}) collective-permute-start(s32[4]{0:T(128)} %multiply_add_fusion.3), channel_id=1, source_target_pairs={{15,0},{0,1},{1,2},{2,3},{3,4},{4,5},{5,6},{6,7},{7,8},{8,9},{9,10... | collective-permute-start | bytes 56 | tf_op jit(solution)/shard_map/ppermute | solution.py:16
  5.0 2.0 %convolution_convert_fusion.6 = bf16[4,32,768]{2,0,1:T(4,128)(2,1)} fusion(s32[8]{0:T(128)S(1)} %get-tuple-element.70, bf16[1,8,32,768]{3,2,1,0:T(8,128)(2,1)} %bitcast.130), kind=kOutput, calls=%fused_computation.47 | convolution fusion | flops 1671264 | bytes 589856 | tf_op jit(solution)/shard_map/dot_general | solution.py:147
  8.1 1.3 %convolution_convert_fusion.5 = bf16[4,32,768]{2,0,1:T(4,128)(2,1)S(1)} fusion(s32[8]{0:T(128)S(1)} %get-tuple-element.69, bf16[1,8,32,768]{3,2,1,0:T(8,128)(2,1)} %bitcast.131), kind=kOutput, calls=%fused_computation.46 | convolution fusion | flops 1671264 | bytes 589856 | tf_op jit(solution)/shard_map/dot_general | solution.py:147
  13.5 6.4 %all-to-all-start = ((s32[16,1,12]{2,1,0:T(1,128)}), s32[16,1,12]{2,1,0:T(1,128)S(1)}, u32[]{:S(2)}, u32[]{:S(2)}) async-start(s32[16,1,12]{2,1,0:T(1,128)} %bitcast.18), calls=%async_computation | async-start | bytes 16384 | tf_op jit(solution)/shard_map/all_to_all | solution.py:129
  20.9 1.5 %collective-permute-start.6 = (bf16[4,31,768]{2,0,1:T(4,128)(2,1)}, bf16[4,31,768]{2,0,1:T(4,128)(2,1)}, u32[]{:S(2)}, u32[]{:S(2)}) collective-permute-start(bf16[4,31,768]{2,0,1:T(4,128)(2,1)} %convolution_convert_fusion.10), channel_id=1, source_target_pairs={{15,0},{0,1},{1,2},{2,3},{3,4},{4,5},{5,6},{6,7},{7,8},{8,9},{9,10... | collective-permute-start | bytes 571400 | tf_op jit(solution)/shard_map/ppermute | solution.py:16
  23.0 1.0 %convolution_convert_fusion.8 = bf16[4,32,768]{2,0,1:T(4,128)(2,1)} fusion(s32[8]{0:T(128)S(1)} %get-tuple-element.70, bf16[1,8,32,768]{3,2,1,0:T(8,128)(2,1)S(1)} %bitcast.134), kind=kOutput, calls=%fused_computation.49 | convolution fusion | flops 1671264 | bytes 589856 | tf_op jit(solution)/shard_map/dot_general | solution.py:147
  24.0 1.0 %convolution_convert_fusion.7 = bf16[4,32,768]{2,0,1:T(4,128)(2,1)} fusion(s32[8]{0:T(128)S(1)} %get-tuple-element.69, bf16[1,8,32,768]{3,2,1,0:T(8,128)(2,1)S(1)} %bitcast.135), kind=kOutput, calls=%fused_computation.48 | convolution fusion | flops 1671264 | bytes 589856 | tf_op jit(solution)/shard_map/dot_general | solution.py:147
  25.2 1.1 %fusion.54 = f32[8,31,768]{2,0,1:T(8,128)} fusion(bf16[8,31,768]{2,0,1:T(8,128)(2,1)S(1)} %copy-done.3, s32[8]{0:T(128)S(1)} %get-tuple-element.71), kind=kOutput, calls=%fused_computation.109 | convolution fusion | flops 3047488 | bytes 1142816 | tf_op jit(solution)/shard_map/dot_general | solution.py:147
  29.8 1.0 %reshape.589 = bf16[16,12,1536]{2,1,0:T(8,128)(2,1)} reshape(bf16[192,1536]{1,0:T(8,128)(2,1)S(1)} %convolution_convert_fusion.1) | data formatting | bytes 1179648 | tf_op jit(solution)/shard_map/reshape | solution.py:125
  31.5 4.9 %all-to-all-start.1 = ((bf16[16,12,1536]{2,1,0:T(8,128)(2,1)}), bf16[16,12,1536]{2,1,0:T(8,128)(2,1)S(1)}, u32[]{:S(2)}, u32[]{:S(2)}) async-start(bf16[16,12,1536]{2,1,0:T(8,128)(2,1)} %reshape.589), calls=%async_computation.1 | async-start | bytes 1572864 | tf_op jit(solution)/shard_map/all_to_all | solution.py:127
  37.5 1.5 %collective-permute-start.1 = (bf16[4,32,768]{2,0,1:T(4,128)(2,1)}, bf16[4,32,768]{2,0,1:T(4,128)(2,1)S(1)}, u32[]{:S(2)}, u32[]{:S(2)}) collective-permute-start(bf16[4,32,768]{2,0,1:T(4,128)(2,1)} %convolution_convert_fusion.8), channel_id=1, source_target_pairs={{15,0},{0,1},{1,2},{2,3},{3,4},{4,5},{5,6},{6,7},{7,8},{8,9},{9,10... | collective-permute-start | bytes 589832 | tf_op jit(solution)/shard_map/ppermute | solution.py:16
  39.0 1.6 %convolution_add_fusion.5 = f32[8,31,768]{2,0,1:T(8,128)S(1)} fusion(f32[8,31,768]{2,0,1:T(8,128)} %fusion.54, bf16[4,31,768]{2,0,1:T(4,128)(2,1)} %collective-permute-done.6, s32[4]{0:T(128)} %collective-permute-done), kind=kOutput, calls=%fused_computation.34 | convolution fusion | flops 1714208 | bytes 1714192 | tf_op jit(solution)/shard_map/dot_general | solution.py:147
  41.6 16.1 %collective-permute-done.7 = bf16[4,31,768]{2,0,1:T(4,128)(2,1)S(1)} collective-permute-done((bf16[4,31,768]{2,0,1:T(4,128)(2,1)S(1)}, bf16[4,31,768]{2,0,1:T(4,128)(2,1)S(1)}, u32[]{:S(2)}, u32[]{:S(2)}) %collective-permute-start.7) | collective-permute-done | bytes 190496 | tf_op jit(solution)/shard_map/ppermute | solution.py:16
  57.7 1.0 %fusion.13 = bf16[8,31,768]{2,0,1:T(8,128)(2,1)S(1)} fusion(f32[8,31,768]{2,0,1:T(8,128)S(1)} %convolution_add_fusion.5, bf16[4,31,768]{2,0,1:T(4,128)(2,1)S(1)} %collective-permute-done.7, s32[4]{0:T(128)} %collective-permute-done.2), kind=kOutput, calls=%fused_computation.40 | convolution fusion | flops 1904672 | bytes 1333264 | tf_op jit(solution)/shard_map/dot_general | solution.py:147
  58.7 1.3 %convolution_add_fusion.1 = f32[8,32,768]{2,0,1:T(8,128)S(1)} fusion(f32[8,32,768]{2,0,1:T(8,128)S(1)} %fusion.87, bf16[4,32,768]{2,0,1:T(4,128)(2,1)} %collective-permute-done.4, s32[4]{0:T(128)} %collective-permute-done), kind=kOutput, calls=%fused_computation.29 | convolution fusion | flops 1769504 | bytes 1769488 | tf_op jit(solution)/shard_map/dot_general | solution.py:147
  60.0 1.0 %convolution_add_fusion.3 = f32[8,32,768]{2,0,1:T(8,128)S(1)} fusion(f32[8,32,768]{2,0,1:T(8,128)S(1)} %fusion.89, bf16[4,32,768]{2,0,1:T(4,128)(2,1)S(1)} %collective-permute-done.1, s32[4]{0:T(128)} %collective-permute-done), kind=kOutput, calls=%fused_computation.31 | convolution fusion | flops 1769504 | bytes 1769488 | tf_op jit(solution)/shard_map/dot_general | solution.py:147
  61.1 1.0 %fusion.12 = bf16[8,32,768]{2,0,1:T(8,128)(2,1)S(1)} fusion(f32[8,32,768]{2,0,1:T(8,128)S(1)} %convolution_add_fusion.1, bf16[4,32,768]{2,0,1:T(4,128)(2,1)S(1)} %collective-permute-done.5, s32[4]{0:T(128)} %collective-permute-done.2), kind=kOutput, calls=%fused_computation.36 | convolution fusion | flops 1966112 | bytes 1376272 | tf_op jit(solution)/shard_map/dot_general | solution.py:147
  62.1 1.8 %fusion.11 = bf16[8,32,768]{2,0,1:T(8,128)(2,1)} fusion(f32[8,32,768]{2,0,1:T(8,128)S(1)} %convolution_add_fusion.3, bf16[4,32,768]{2,0,1:T(4,128)(2,1)S(1)} %collective-permute-done.3, s32[4]{0:T(128)} %collective-permute-done.2), kind=kOutput, calls=%fused_computation.35 | convolution fusion | flops 1966112 | bytes 1376272 | tf_op jit(solution)/shard_map/dot_general | solution.py:147
  64.8 4.8 %fusion.3 = bf16[16,12,2304]{2,0,1:T(8,128)(2,1)S(1)} fusion(bf16[1536,2304]{1,0:T(8,128)(2,1)} %param.18, bf16[16,12,1536]{2,1,0:T(8,128)(2,1)S(1)} %fusion.9), kind=kOutput, calls=%fused_computation.3 | convolution fusion | flops 1359396864 | bytes 8552448 | tf_op jit(solution)/shard_map/...d,de->...e/dot_general | solution.py:27
  72.3 1.7 %reshape.592 = bf16[8,48,8,96]{3,2,0,1:T(8,128)(2,1)} reshape(bf16[8,48,768]{2,0,1:T(8,128)(2,1)S(1)} %pad_maximum_fusion.2) | data formatting | bytes 1179648 | tf_op jit(solution)/shard_map/reshape | solution.py:48
  74.0 1.1 %convolution_convert_fusion.4 = bf16[8,32,768]{2,1,0:T(8,128)(2,1)} fusion(bf16[8,48,768]{2,0,1:T(8,128)(2,1)S(1)} %pad_maximum_fusion.1, s32[8,32]{1,0:T(8,128)S(1)} %iota_add_fusion.1), kind=kOutput, calls=%fused_computation.39 | convolution fusion | flops 19083264 | bytes 984064 | tf_op jit(solution)/shard_map/sij,sjc->sic/dot_general | solution.py:33
  75.1 1.1 %convolution_convert_fusion.3 = bf16[8,32,768]{2,1,0:T(8,128)(2,1)} fusion(bf16[8,48,768]{2,0,1:T(8,128)(2,1)S(1)} %pad_maximum_fusion.2, s32[8,32]{1,0:T(8,128)S(1)} %iota_add_fusion.1), kind=kOutput, calls=%fused_computation.38 | convolution fusion | flops 19083264 | bytes 984064 | tf_op jit(solution)/shard_map/sij,sjc->sic/dot_general | solution.py:33
  77.5 1.9 %fusion.17 = bf16[8,16,8,96]{3,1,2,0:T(8,128)(2,1)S(1)} fusion(bf16[8,48,8,96]{3,2,0,1:T(8,128)(2,1)S(1)} %copy-done.6, f32[8,8,16]{2,1,0:T(8,128)S(1)} %fusion.120, pred[8,16]{1,0:T(8,128)(4,1)S(1)} %copy-done.45, f32[8,8,16,48]{3,2,1,0:T(8,128)S(1)} %fusion.15), kind=kOutput, calls=%fused_computation.52 | convolution fusion | flops 9782319 | bytes 987264 | tf_op jit(solution)/shard_map/shqk,skhd->sqhd/dot_general | solution.py:63
  81.7 5.4 %fusion.51 = bf16[8,16,768]{2,0,1:T(8,128)(2,1)S(1)} fusion(bf16[8,16,768]{2,0,1:T(8,128)(2,1)S(1)} %copy.81, bf16[8,31,768]{2,0,1:T(8,128)(2,1)S(1)} %fusion.13, f32[768]{0:T(1024)S(1)} %copy-done.40, f32[768]{0:T(1024)S(1)} %copy-done.41, f32[768]{0:T(1024)S(1)} %copy-done.11, f32[768]{0:T(1024)S(1)} %copy-done.12, f32[768]{0:T(1024)S(1)} %copy-done.13, ...), kind=kLoop, calls=%fused_computation.106 | loop fusion | flops 11108352 | bytes 4052992 | tf_op jit(solution)/shard_map/convert_element_type | solution.py:76
  (164 shorter events, 22.9 us)
Async XLA Ops:
  0.6 27.4 %copy-start = (bf16[128,1536]{1,0:T(8,128)(2,1)S(1)}, bf16[128,1536]{1,0:T(8,128)(2,1)}, u32[]{:S(2)}) copy-start(bf16[128,1536]{1,0:T(8,128)(2,1)} %param.10) | copy-start | bytes 1179652
  0.6 21.7 %copy-start.1 = (bf16[8,32,768]{2,1,0:T(8,128)(2,1)S(1)}, bf16[8,32,768]{2,1,0:T(8,128)(2,1)}, u32[]{:S(2)}) copy-start(bf16[8,32,768]{2,1,0:T(8,128)(2,1)} %param.15) | copy-start | bytes 1179652
  0.7 19.3 %copy-start.3 = (bf16[8,31,768]{2,0,1:T(8,128)(2,1)S(1)}, bf16[8,31,768]{2,0,1:T(8,128)(2,1)}, u32[]{:S(2)}) copy-start(bf16[8,31,768]{2,0,1:T(8,128)(2,1)} %param.17) | copy-start | bytes 1142788
  3.2 34.3 %collective-permute-start = (s32[4]{0:T(128)}, s32[4]{0:T(128)}, u32[]{:S(2)}, u32[]{:S(2)}) collective-permute-start(s32[4]{0:T(128)} %multiply_add_fusion.3), channel_id=1, source_target_pairs={{15,0},{0,1},{1,2},{2,3},{3,4},{4,5},{5,6},{6,7},{7,8},{8,9},{9,10... | collective-permute-start | bytes 56 | tf_op jit(solution)/shard_map/ppermute | solution.py:16
  5.0 17.7 %copy-start.2 = (bf16[8,32,768]{2,1,0:T(8,128)(2,1)S(1)}, bf16[8,32,768]{2,1,0:T(8,128)(2,1)}, u32[]{:S(2)}) copy-start(bf16[8,32,768]{2,1,0:T(8,128)(2,1)} %param.16) | copy-start | bytes 1179652
  7.1 51.6 %collective-permute-start.4 = (bf16[4,32,768]{2,0,1:T(4,128)(2,1)}, bf16[4,32,768]{2,0,1:T(4,128)(2,1)}, u32[]{:S(2)}, u32[]{:S(2)}) collective-permute-start(bf16[4,32,768]{2,0,1:T(4,128)(2,1)} %convolution_convert_fusion.6), channel_id=1, source_target_pairs={{15,0},{0,1},{1,2},{2,3},{3,4},{4,5},{5,6},{6,7},{7,8},{8,9},{9,10... | collective-permute-start | bytes 589832 | tf_op jit(solution)/shard_map/ppermute | solution.py:16
  7.6 33.0 %collective-permute-start.2 = (s32[4]{0:T(128)}, s32[4]{0:T(128)}, u32[]{:S(2)}, u32[]{:S(2)}) collective-permute-start(s32[4]{0:T(128)} %multiply_add_fusion.2), channel_id=1, source_target_pairs={{1,0},{2,1},{3,2},{4,3},{5,4},{6,5},{7,6},{8,7},{9,8},{10,9},{11,1... | collective-permute-start | bytes 56 | tf_op jit(solution)/shard_map/ppermute | solution.py:16
  9.4 51.6 %collective-permute-start.5 = (bf16[4,32,768]{2,0,1:T(4,128)(2,1)S(1)}, bf16[4,32,768]{2,0,1:T(4,128)(2,1)S(1)}, u32[]{:S(2)}, u32[]{:S(2)}) collective-permute-start(bf16[4,32,768]{2,0,1:T(4,128)(2,1)S(1)} %convolution_convert_fusion.5), channel_id=1, source_target_pairs={{1,0},{2,1},{3,2},{4,3},{5,4},{6,5},{7,6},{8,7},{9,8},{10,9},{11,1... | collective-permute-start | bytes 589832 | tf_op jit(solution)/shard_map/ppermute | solution.py:16
  13.5 18.0 %all-to-all-start = ((s32[16,1,12]{2,1,0:T(1,128)}), s32[16,1,12]{2,1,0:T(1,128)S(1)}, u32[]{:S(2)}, u32[]{:S(2)}) async-start(s32[16,1,12]{2,1,0:T(1,128)} %bitcast.18), calls=%async_computation | async-start | bytes 16384 | tf_op jit(solution)/shard_map/all_to_all | solution.py:129
  20.9 18.2 %collective-permute-start.6 = (bf16[4,31,768]{2,0,1:T(4,128)(2,1)}, bf16[4,31,768]{2,0,1:T(4,128)(2,1)}, u32[]{:S(2)}, u32[]{:S(2)}) collective-permute-start(bf16[4,31,768]{2,0,1:T(4,128)(2,1)} %convolution_convert_fusion.10), channel_id=1, source_target_pairs={{15,0},{0,1},{1,2},{2,3},{3,4},{4,5},{5,6},{6,7},{7,8},{8,9},{9,10... | collective-permute-start | bytes 571400 | tf_op jit(solution)/shard_map/ppermute | solution.py:16
  22.4 2.7 %copy-start.43 = (s32[8]{0:T(128)S(1)}, s32[8]{0:T(128)}, u32[]{:S(2)}) copy-start(s32[8]{0:T(128)} %param.14) | copy-start | bytes 100
  24.0 4.3 %copy-start.7 = (bf16[32,768]{1,0:T(8,128)(2,1)S(1)}, bf16[32,768]{1,0:T(8,128)(2,1)}, u32[]{:S(2)}) copy-start(bf16[32,768]{1,0:T(8,128)(2,1)} %param.19) | copy-start | bytes 147460
  25.2 5.6 %copy-start.44 = (pred[8,16]{1,0:T(8,128)(4,1)}, pred[8,16]{1,0:T(8,128)(4,1)S(1)}, u32[]{:S(2)}) copy-start(pred[8,16]{1,0:T(8,128)(4,1)S(1)} %iota_compare_fusion.11) | copy-start | bytes 388
  28.3 10.7 %copy-start.8 = (bf16[4,31,768]{2,0,1:T(4,128)(2,1)S(1)}, bf16[4,31,768]{2,0,1:T(4,128)(2,1)}, u32[]{:S(2)}) copy-start(bf16[4,31,768]{2,0,1:T(4,128)(2,1)} %convolution_convert_fusion.9) | copy-start | bytes 571396
  31.5 32.4 %all-to-all-start.1 = ((bf16[16,12,1536]{2,1,0:T(8,128)(2,1)}), bf16[16,12,1536]{2,1,0:T(8,128)(2,1)S(1)}, u32[]{:S(2)}, u32[]{:S(2)}) async-start(bf16[16,12,1536]{2,1,0:T(8,128)(2,1)} %reshape.589), calls=%async_computation.1 | async-start | bytes 1572864 | tf_op jit(solution)/shard_map/all_to_all | solution.py:127
  37.5 22.5 %collective-permute-start.1 = (bf16[4,32,768]{2,0,1:T(4,128)(2,1)}, bf16[4,32,768]{2,0,1:T(4,128)(2,1)S(1)}, u32[]{:S(2)}, u32[]{:S(2)}) collective-permute-start(bf16[4,32,768]{2,0,1:T(4,128)(2,1)} %convolution_convert_fusion.8), channel_id=1, source_target_pairs={{15,0},{0,1},{1,2},{2,3},{3,4},{4,5},{5,6},{6,7},{7,8},{8,9},{9,10... | collective-permute-start | bytes 589832 | tf_op jit(solution)/shard_map/ppermute | solution.py:16
  39.0 18.6 %collective-permute-start.7 = (bf16[4,31,768]{2,0,1:T(4,128)(2,1)S(1)}, bf16[4,31,768]{2,0,1:T(4,128)(2,1)S(1)}, u32[]{:S(2)}, u32[]{:S(2)}) collective-permute-start(bf16[4,31,768]{2,0,1:T(4,128)(2,1)S(1)} %copy-done.8), channel_id=1, source_target_pairs={{1,0},{2,1},{3,2},{4,3},{5,4},{6,5},{7,6},{8,7},{9,8},{10,9},{11,1... | collective-permute-start | bytes 571400 | tf_op jit(solution)/shard_map/ppermute | solution.py:16
  40.6 21.5 %collective-permute-start.3 = (bf16[4,32,768]{2,0,1:T(4,128)(2,1)}, bf16[4,32,768]{2,0,1:T(4,128)(2,1)S(1)}, u32[]{:S(2)}, u32[]{:S(2)}) collective-permute-start(bf16[4,32,768]{2,0,1:T(4,128)(2,1)} %convolution_convert_fusion.7), channel_id=1, source_target_pairs={{1,0},{2,1},{3,2},{4,3},{5,4},{6,5},{7,6},{8,7},{9,8},{10,9},{11,1... | collective-permute-start | bytes 589832 | tf_op jit(solution)/shard_map/ppermute | solution.py:16
  72.3 3.9 %copy-start.5 = (bf16[8,16,768]{2,1,0:T(8,128)(2,1)S(1)}, bf16[8,16,768]{2,1,0:T(8,128)(2,1)}, u32[]{:S(2)}) copy-start(bf16[8,16,768]{2,1,0:T(8,128)(2,1)} %get-tuple-element.66) | copy-start | bytes 589828
  75.1 2.4 %copy-start.45 = (pred[8,16]{1,0:T(8,128)(4,1)S(1)}, pred[8,16]{1,0:T(8,128)(4,1)}, u32[]{:S(2)}) copy-start(pred[8,16]{1,0:T(8,128)(4,1)} %copy-done.44) | copy-start | bytes 388
  79.7 1.7 %copy-start.10 = (f32[768]{0:T(1024)S(1)}, f32[768]{0:T(1024)}, u32[]{:S(2)}) copy-start(f32[768]{0:T(1024)} %get-tuple-element.24) | copy-start | bytes 9220
  79.7 1.7 %copy-start.11 = (f32[768]{0:T(1024)S(1)}, f32[768]{0:T(1024)}, u32[]{:S(2)}) copy-start(f32[768]{0:T(1024)} %get-tuple-element.25) | copy-start | bytes 9220
  79.7 1.7 %copy-start.12 = (f32[768]{0:T(1024)S(1)}, f32[768]{0:T(1024)}, u32[]{:S(2)}) copy-start(f32[768]{0:T(1024)} %get-tuple-element.26) | copy-start | bytes 9220
  79.7 1.7 %copy-start.13 = (f32[768]{0:T(1024)S(1)}, f32[768]{0:T(1024)}, u32[]{:S(2)}) copy-start(f32[768]{0:T(1024)} %get-tuple-element.27) | copy-start | bytes 9220
  (32 other events, 51.3 us)
where the time goes:
time: 88.4 us; the launch traced here: 87.8 us
  matrix products  27.1 us (31%)
  starting transfers between devices  17.7 us (20%)
  waiting for transfers between devices  16.1 us (18%)
  other arithmetic  16 us (18%)
  local copies, waits for them, and re-layouts  9.31 us (11%)
  between operations  1.55 us (2%)
    dot_general x15, matrix products, apply_rows(): result = jnp.dot(selector, flat_state, preferred_element_type=jnp.float32)  16.8 us
    ppermute x8, waiting for transfers between devices, from_behind(): return lax.ppermute(block, axis, route)  16.1 us
    all_to_all x1, starting transfers between devices, local(): lax.all_to_all(where_to, 'streams', split_axis=0, concat_axis=0, tiled=True)  6.42 us
    ppermute x8, starting transfers between devices, from_behind(): return lax.ppermute(block, axis, route)  6.37 us
    convert_element_type x1, other arithmetic, stream_step(): jnp.where(alive_rows[:, :, None], summed, 0.0).astype(jnp.bfloat16)  5.39 us
    all_to_all x1, starting transfers between devices, local(): lax.all_to_all(outgoing, 'streams', split_axis=0, concat_axis=0, tiled=True)  4.87 us
    dot_general x1, matrix products, project(): jnp.einsum('...d,de->...e', layer_norm(payload), qkv_weight, preferred_el...  4.78 us
    dot_general x3, matrix products, select_rows(): jnp.einsum('sij,sjc->sic', selector, source, preferred_element_type=jnp.f...  2.44 us
  transfers between devices with their start and end apart: 10, of which 1 were waited for; matrix products, arithmetic and copies ran while one was open for 30% of the time, Pallas kernels for 0%

commit v1 on v0

v1 whole, which is shorter than its diff:
```python
import jax
import jax.numpy as jnp
from jax import lax
from jax.experimental import pallas as pl
from jax.experimental.pallas import tpu as pltpu
from jax.sharding import PartitionSpec as P

HEAD = 96
MIG = 4
EPSILON = 1e-05
LANES = 128
TILE = 8
FOLD = 2

BF16 = jnp.bfloat16
F32 = jnp.float32
I32 = jnp.int32


def iota(shape, axis):
    return lax.broadcasted_iota(I32, shape, axis)


def ones_where(condition):
    return jnp.where(condition, 1.0, 0.0).astype(BF16)


def matmul(left, right):
    return jnp.dot(left, right, preferred_element_type=F32)


def matmul_nt(left, right):
    return lax.dot_general(left, right, (((1,), (1,)), ((), ())), preferred_element_type=F32)


def round_up(value, multiple):
    return -(-value // multiple) * multiple


def whole(*spaces):
    return [pl.BlockSpec(memory_space=space) for space in spaces]


def block_sizes(width, capacity):
    slots = round_up(capacity, TILE // FOLD)
    group_rows = FOLD * slots
    groups = width // FOLD // LANES
    return slots, group_rows, groups, groups * group_rows + TILE


def pack_frames(frames, route_peer, route_pos, peers, capacity):
    row_count, width = frames.shape
    slots, group_rows, groups, block_rows = block_sizes(width, capacity)
    half = width // FOLD

    def body(frames_ref, peer_ref, pos_ref, out_ref):
        peer = peer_ref[...]
        owner = ones_where(iota((peers, row_count), 0) == peer)
        earlier = ones_where(iota((row_count, row_count), 0) < iota((row_count, row_count), 1))
        running = matmul(owner, earlier)
        slot = jnp.sum(running * owner.astype(F32), axis=0, keepdims=True).astype(I32)
        flat = peer * group_rows + slot
        rows = iota((peers * group_rows, row_count), 0)
        pick = jnp.concatenate([ones_where(rows == flat + h * slots) for h in range(FOLD)], axis=1)
        source = jnp.concatenate(
            [frames_ref[:, h * half : (h + 1) * half] for h in range(FOLD)], axis=0
        )
        packed = matmul(pick, source).astype(BF16)
        owner_tile = ones_where(iota((peers * TILE, row_count), 0) // TILE == peer)
        lane = iota((LANES, row_count), 0)
        in_lane = (lane % slots == slot) & (lane < group_rows)
        code = jnp.where(in_lane, (pos_ref[...] + 1).astype(F32), 0.0).astype(BF16)
        codes = matmul_nt(owner_tile, code).astype(BF16)
        for p in range(peers):
            for g in range(groups):
                out_ref[p * block_rows + g * group_rows : p * block_rows + (g + 1) * group_rows, :] = (
                    packed[p * group_rows : (p + 1) * group_rows, g * LANES : (g + 1) * LANES]
                )
            out_ref[(p + 1) * block_rows - TILE : (p + 1) * block_rows, :] = codes[
                p * TILE : (p + 1) * TILE, :
            ]

    return pl.pallas_call(
        body,
        out_shape=jax.ShapeDtypeStruct((peers * block_rows, LANES), BF16),
        in_specs=whole(pltpu.VMEM, pltpu.VMEM, pltpu.VMEM),
        out_specs=pl.BlockSpec(memory_space=pltpu.VMEM),
        name="pack_frames",
    )(frames, route_peer.reshape(1, -1), route_pos.reshape(1, -1))


def pack_streams(destination, key_cache, value_cache, conv_state, peers):
    streams, left, width = key_cache.shape
    tail = conv_state.shape[1]
    rows = 2 * left + 1 + tail

    def body(dest_ref, own_ref, key_ref, value_ref, conv_ref, up_ref, down_ref):
        own = own_ref[0]
        up_ref[...] = jnp.zeros_like(up_ref)
        down_ref[...] = jnp.zeros_like(down_ref)

        def put(out_ref, rank, j, slot):
            out_ref[rank, 0:left, :] = key_ref[j]
            out_ref[rank, left : 2 * left, :] = value_ref[j]
            code = jnp.full((1, width), slot + 1, I32).astype(F32).astype(BF16)
            out_ref[rank, 2 * left : rows, :] = jnp.concatenate([code, conv_ref[j]], axis=0)

        def step(chosen_device, out_ref):
            rank = jnp.int32(0)
            for j in range(streams):
                target = dest_ref[j]
                chosen = target // streams == chosen_device

                @pl.when(chosen)
                def _():
                    put(out_ref, jnp.minimum(rank, MIG - 1), j, target % streams)

                rank = rank + chosen.astype(I32)

        step((own + 1) % peers, up_ref)
        step((own + peers - 1) % peers, down_ref)

    bundle = jax.ShapeDtypeStruct((MIG, rows, width), BF16)
    return pl.pallas_call(
        body,
        out_shape=(bundle, bundle),
        in_specs=whole(pltpu.SMEM, pltpu.SMEM, pltpu.VMEM, pltpu.VMEM, pltpu.VMEM),
        out_specs=whole(pltpu.VMEM, pltpu.VMEM),
        name="pack_streams",
    )(destination, own_index(), key_cache, value_cache, conv_state)


def own_index():
    return lax.axis_index("streams").astype(I32).reshape(1)


def stream_step(
    received, from_lower, from_upper, destination, valid_count, key_cache, value_cache, conv_state,
    qkv_weight, conv_kernel, peers, row_count, capacity,
):
    streams, left, width = key_cache.shape
    tail = conv_state.shape[1]
    taps = conv_kernel.shape[0]
    span = row_count // streams
    model = qkv_weight.shape[0]
    half = model // FOLD
    heads = width // HEAD
    keys = left + span
    window = 1 + tail + span
    slots, group_rows, groups, block_rows = block_sizes(model, capacity)
    packed_rows = peers * group_rows

    def body(
        dest_ref, own_ref, valid_ref, recv_ref, lower_ref, upper_ref, key_ref, value_ref, conv_ref,
        weight_ref, taps_ref, encoded_ref, keys_next_ref, values_next_ref, conv_next_ref,
        gathered, keys_all, values_all, conv_in, taps_f32, encoded_f32,
    ):
        own = own_ref[0]
        for j in range(streams):
            target = dest_ref[j]

            @pl.when(target // streams == own)
            def _():
                slot = target % streams
                keys_all[slot, 0:left, :] = key_ref[j]
                values_all[slot, 0:left, :] = value_ref[j]
                conv_in[slot, 1 : 1 + tail, :] = conv_ref[j].astype(F32)

        for bundle_ref in (lower_ref, upper_ref):
            for j in range(MIG):
                code = jnp.max(bundle_ref[j, 2 * left : 2 * left + 1, :].astype(F32)).astype(I32)

                @pl.when(code > 0)
                def _():
                    keys_all[code - 1, 0:left, :] = bundle_ref[j, 0:left, :]
                    values_all[code - 1, 0:left, :] = bundle_ref[j, left : 2 * left, :]
                    conv_in[code - 1, 0 : 1 + tail, :] = bundle_ref[
                        j, 2 * left : 2 * left + 1 + tail, :
                    ].astype(F32)

        for p in range(peers):
            for g in range(groups):
                gathered[p * group_rows : (p + 1) * group_rows, g * LANES : (g + 1) * LANES] = recv_ref[
                    p * block_rows + g * group_rows : p * block_rows + (g + 1) * group_rows, :
                ]
        codes = jnp.concatenate(
            [recv_ref[(p + 1) * block_rows - TILE : (p + 1) * block_rows, :] for p in range(peers)],
            axis=0,
        )
        spread_lane = ones_where(
            iota((LANES, packed_rows), 1) % group_rows == iota((LANES, packed_rows), 0)
        )
        spread = matmul(codes, spread_lane)
        column = iota((peers * TILE, packed_rows), 1)
        own_tile = iota((peers * TILE, packed_rows), 0) == column // group_rows * TILE
        position = jnp.sum(jnp.where(own_tile, spread, 0.0), axis=0, keepdims=True).astype(I32)
        out_row = iota((row_count, packed_rows), 0) + 1
        column_half = iota((row_count, packed_rows), 1) % group_rows // slots
        hit = out_row == position
        place = jnp.concatenate([ones_where(hit & (column_half == h)) for h in range(FOLD)], axis=0)
        halves = matmul(place, gathered[...])
        owned = jnp.concatenate(
            [halves[h * row_count : (h + 1) * row_count, :] for h in range(FOLD)], axis=1
        )
        centered = owned - jnp.mean(owned, axis=-1, keepdims=True)
        spread_of = jnp.mean(centered * centered, axis=-1, keepdims=True)
        normed = (centered * lax.rsqrt(spread_of + EPSILON)).astype(BF16)
        qkv = matmul(normed, weight_ref[...]).astype(BF16)

        head_rows = heads * span
        lane_head = iota((head_rows, width), 1) // HEAD
        head_mask = ones_where(lane_head == iota((head_rows, width), 0) // span)
        t_of = iota((head_rows, keys), 0) % span
        key_of = iota((head_rows, keys), 1) - left
        t_row = iota((span, width), 0)
        lane_head16 = iota((span, width), 1) // HEAD
        pick_row = iota((left, keys), 0)
        pick_col = iota((left, keys), 1)
        conv_row = iota((tail, window), 0)
        conv_col = iota((tail, window), 1)
        for s in range(streams):
            valid = valid_ref[s]
            row = slice(s * span, (s + 1) * span)
            keys_all[s, left:keys, :] = qkv[row, width : 2 * width]
            values_all[s, left:keys, :] = qkv[row, 2 * width : 3 * width]
            queries = jnp.concatenate([qkv[row, 0:width]] * heads, axis=0) * head_mask
            scores = matmul_nt(queries, keys_all[s]) * HEAD ** (-0.5)
            allowed = (key_of < 0) | ((key_of <= t_of) & (key_of < valid))
            scores = jnp.where(allowed, scores, -1e30)
            weights = jnp.exp(scores - jnp.max(scores, axis=-1, keepdims=True))
            probabilities = (weights / jnp.sum(weights, axis=-1, keepdims=True)).astype(BF16)
            mixed = matmul(probabilities, values_all[s])
            attended = mixed[0:span, :]
            for h in range(1, heads):
                attended = jnp.where(lane_head16 == h, mixed[h * span : (h + 1) * span, :], attended)
            attended = jnp.where(t_row < valid, attended, 0.0).astype(BF16)
            conv_in[s, 1 + tail : window, :] = attended.astype(F32)
            pick = ones_where(pick_col == pick_row + valid)
            keys_next_ref[s] = matmul(pick, keys_all[s]).astype(BF16)
            values_next_ref[s] = matmul(pick, values_all[s]).astype(BF16)
            conv_pick = ones_where(conv_col == conv_row + (valid + 1))
            conv_next_ref[s] = matmul(conv_pick, conv_in[s].astype(BF16)).astype(BF16)

        taps_f32[...] = taps_ref[...].astype(F32)
        stream_of = iota((streams, LANES), 0)
        valid_rows = jnp.zeros((streams, LANES), I32)
        for s in range(streams):
            valid_rows = jnp.where(stream_of == s, valid_ref[s], valid_rows)
        for c in range(width // LANES):
            lanes = slice(c * LANES, (c + 1) * LANES)
            inputs = [conv_in[:, 1 + j, lanes] for j in range(tail + span)]
            for t in range(span):
                total = inputs[tail + t]
                for i in range(taps):
                    total = total + taps_f32[i : i + 1, lanes] * inputs[t + i]
                encoded_f32[:, t, lanes] = jnp.where(t < valid_rows, total, 0.0)
        encoded_ref[...] = encoded_f32[...].reshape(row_count, width).astype(BF16)

    out_shape = (
        jax.ShapeDtypeStruct((row_count, width), BF16),
        jax.ShapeDtypeStruct((streams, left, width), BF16),
        jax.ShapeDtypeStruct((streams, left, width), BF16),
        jax.ShapeDtypeStruct((streams, tail, width), BF16),
    )
    return pl.pallas_call(
        body,
        out_shape=out_shape,
        in_specs=whole(*[pltpu.SMEM] * 3, *[pltpu.VMEM] * 8),
        out_specs=whole(*[pltpu.VMEM] * 4),
        scratch_shapes=[
            pltpu.VMEM((packed_rows, half), BF16),
            pltpu.VMEM((streams, keys, width), BF16),
            pltpu.VMEM((streams, keys, width), BF16),
            pltpu.VMEM((streams, window, width), F32),
            pltpu.VMEM((taps, width), F32),
            pltpu.VMEM((streams, span, width), F32),
        ],
        name="stream_step",
    )(
        destination, own_index(), valid_count, received, from_lower, from_upper, key_cache,
        value_cache, conv_state, qkv_weight, conv_kernel,
    )


def from_behind(block, axis, distance):
    count = lax.axis_size(axis)
    return lax.ppermute(block, axis, [((i - distance) % count, i) for i in range(count)])


def local(
    frames, route_peer, route_pos, destination, valid_count, key_cache, value_cache, conv_state,
    qkv_weight, conv_kernel,
):
    peers = lax.axis_size("streams")
    row_count = frames.shape[0]
    per_peer = row_count // peers
    capacity = per_peer + per_peer // 2
    up, down = pack_streams(destination, key_cache, value_cache, conv_state, peers)
    from_lower = from_behind(up, "streams", 1)
    from_upper = from_behind(down, "streams", -1)
    packed = pack_frames(frames, route_peer, route_pos, peers, capacity)
    received = lax.all_to_all(packed, "streams", split_axis=0, concat_axis=0, tiled=True)
    return stream_step(
        received, from_lower, from_upper, destination, valid_count, key_cache, value_cache,
        conv_state, qkv_weight, conv_kernel, peers, row_count, capacity,
    )


def solution(mesh):
    rows = P(("groups", "streams"))
    return jax.shard_map(
        local,
        mesh=mesh,
        in_specs=(rows,) * 8 + (P(), P()),
        out_specs=(rows,) * 4,
        check_vma=False,
    )
```

time: 88.4 us -> 51.7 us (0.58)
  the two profiles are of different devices: /device:TPU:15 before, /device:TPU:1 now
where the time goes in v1:
time: 51.7 us; the launch traced here: 51.3 us
  Pallas kernels  18.8 us (36%)
  waiting for transfers between devices  18.2 us (35%)
  starting transfers between devices  8.95 us (17%)
  local copies, waits for them, and re-layouts  4.8 us (9%)
  between operations  0.64 us (1%)
    ppermute x2, waiting for transfers between devices, from_behind(): lax.ppermute(block, axis, [((i - distance) % count, i) for i in range(cou...  18.2 us
    pallas_call x1, Pallas kernels, stream_step(): pl.pallas_call(body, out_shape=out_shape, in_specs=whole(*[pltpu.SMEM] *...  13.9 us
    all_to_all x1, starting transfers between devices, local(): lax.all_to_all(packed, 'streams', split_axis=0, concat_axis=0, tiled=True)  7.34 us
    unnamed x7, local copies, waits for them, and re-layouts  2.85 us
    pallas_call x1, Pallas kernels, pack_streams(): pl.pallas_call(body, out_shape=(bundle, bundle), in_specs=whole(pltpu.SME...  2.63 us
    pallas_call x1, Pallas kernels, pack_frames(): pl.pallas_call(body, out_shape=jax.ShapeDtypeStruct((peers * block_rows,...  2.29 us
    pallas_call x1, local copies, waits for them, and re-layouts, stream_step(): pl.pallas_call(body, out_shape=out_shape, in_specs=whole(*[pltpu.SMEM] *...  1.96 us
    ppermute x2, starting transfers between devices, from_behind(): lax.ppermute(block, axis, [((i - distance) % count, i) for i in range(cou...  1.61 us
  transfers between devices with their start and end apart: 3, of which 2 were waited for; matrix products, arithmetic and copies ran while one was open for 4% of the time, Pallas kernels for 5%

profile of v1, /device:TPU:1, one launch (start us, length us, event | category | flops | bytes accessed | tf_op | source)
XLA Modules:
  0.0 51.3 jit_solution(8430891645925219498)
XLA Ops:
  0.6 2.3 %pack_frames.1 = bf16[2432,128]{1,0:T(8,128)(2,1)} custom-call(bf16[128,1536]{1,0:T(8,128)(2,1)} %frames_ref.1, s32[1,128]{1,0:T(1,128)} %bitcast.7, s32[1,128]{1,0:T(1,128)} %bitcast.8), custom_call_target="tpu_custom_call" | custom-call | tf_op jit(solution)/shard_map/pack_frames/pallas_call | solution.py:83
  2.9 7.3 %all-to-all-start = ((bf16[16,152,128]{2,1,0:T(8,128)(2,1)}), bf16[16,152,128]{2,1,0:T(8,128)(2,1)S(1)}, u32[]{:S(2)}, u32[]{:S(2)}) async-start(bf16[16,152,128]{2,1,0:T(8,128)(2,1)} %bitcast.5), calls=%async_computation | async-start | bytes 1245184 | tf_op jit(solution)/shard_map/all_to_all | solution.py:302
  10.3 1.8 %copy.14.conv_ref = bf16[8,31,768]{2,1,0:T(8,128)(2,1)} copy(bf16[8,31,768]{2,0,1:T(8,128)(2,1)} %param.17) | data formatting | bytes 761856 | tf_op args[7]
  12.1 2.6 %pack_streams.1 = (bf16[4,96,768]{2,1,0:T(8,128)(2,1)}, bf16[4,96,768]{2,1,0:T(8,128)(2,1)}) custom-call(s32[8]{0:T(128)} %dest_ref.3, s32[1]{0:T(128)} %bitcast.own_ref, bf16[8,32,768]{2,1,0:T(8,128)(2,1)} %key_ref.3, bf16[8,32,768]{2,1,0:T(8,128)(2,1)} %value_ref.3, bf16[8,31,768]{2,1,0:T(8,128)(2,1)} %copy.14.conv_ref), custom_call_target="tpu_custom_call" | custom-call | tf_op jit(solution)/shard_map/pack_streams/pallas_call | solution.py:124
  14.7 1.6 %collective-permute-start = (bf16[4,96,768]{2,1,0:T(8,128)(2,1)}, bf16[4,96,768]{2,1,0:T(8,128)(2,1)S(1)}, u32[]{:S(2)}, u32[]{:S(2)}) collective-permute-start(bf16[4,96,768]{2,1,0:T(8,128)(2,1)} %get-tuple-element.6), channel_id=1, source_target_pairs={{15,0},{0,1},{1,2},{2,3},{3,4},{4,5},{5,6},{6,7},{7,8},{8,9},{9,10... | collective-permute-start | bytes 1769480 | tf_op jit(solution)/shard_map/ppermute | solution.py:287
  16.3 0.0 collective-permute-start.1
  16.3 16.3 %collective-permute-done.lower_ref = bf16[4,96,768]{2,1,0:T(8,128)(2,1)S(1)} collective-permute-done((bf16[4,96,768]{2,1,0:T(8,128)(2,1)}, bf16[4,96,768]{2,1,0:T(8,128)(2,1)S(1)}, u32[]{:S(2)}, u32[]{:S(2)}) %collective-permute-start) | collective-permute-done | bytes 589856 | tf_op jit(solution)/shard_map/ppermute | solution.py:287
  32.6 0.0 copy-start.1
  32.6 1.9 %collective-permute-done.1.upper_ref = bf16[4,96,768]{2,1,0:T(8,128)(2,1)S(1)} collective-permute-done((bf16[4,96,768]{2,1,0:T(8,128)(2,1)}, bf16[4,96,768]{2,1,0:T(8,128)(2,1)S(1)}, u32[]{:S(2)}, u32[]{:S(2)}) %collective-permute-start.1) | collective-permute-done | bytes 589856 | tf_op jit(solution)/shard_map/ppermute | solution.py:287
  34.5 0.0 copy-start.2
  34.5 0.0 all-to-all-done
  34.5 0.0 copy-start
  34.5 0.0 copy-done.1
  34.5 0.8 %copy-done.2 = bf16[4,96,768]{2,1,0:T(8,128)(2,1)} copy-done((bf16[4,96,768]{2,1,0:T(8,128)(2,1)}, bf16[4,96,768]{2,1,0:T(8,128)(2,1)S(1)}, u32[]{:S(2)}) %copy-start.2) | copy-done | bytes 589848
  35.3 0.2 copy-done
  35.5 13.9 %stream_step.1 = (bf16[128,768]{1,0:T(8,128)(2,1)}, bf16[8,32,768]{2,1,0:T(8,128)(2,1)}, bf16[8,32,768]{2,1,0:T(8,128)(2,1)}, bf16[8,31,768]{2,1,0:T(8,128)(2,1)}) custom-call(s32[8]{0:T(128)} %dest_ref.3, s32[1]{0:T(128)} %bitcast.own_ref, s32[8]{0:T(128)} %valid_ref.1, bf16[2432,128]{1,0:T(8,128)(2,1)} %bitcast.6, bf16[4,96,768]{2,1,0:T(8,128)(2,1)} %copy-done.1, ...), custom_call_target="tpu_custom_call" | custom-call | tf_op jit(solution)/shard_map/stream_step/pallas_call | solution.py:265
  49.4 2.0 %copy.16 = bf16[8,31,768]{2,0,1:T(8,128)(2,1)} copy(bf16[8,31,768]{2,1,0:T(8,128)(2,1)} %get-tuple-element.11) | data formatting | bytes 761856 | tf_op jit(solution)/shard_map/stream_step/pallas_call | solution.py:265
Async XLA Ops:
  2.9 31.6 %all-to-all-start = ((bf16[16,152,128]{2,1,0:T(8,128)(2,1)}), bf16[16,152,128]{2,1,0:T(8,128)(2,1)S(1)}, u32[]{:S(2)}, u32[]{:S(2)}) async-start(bf16[16,152,128]{2,1,0:T(8,128)(2,1)} %bitcast.5), calls=%async_computation | async-start | bytes 1245184 | tf_op jit(solution)/shard_map/all_to_all | solution.py:302
  14.7 17.9 %collective-permute-start = (bf16[4,96,768]{2,1,0:T(8,128)(2,1)}, bf16[4,96,768]{2,1,0:T(8,128)(2,1)S(1)}, u32[]{:S(2)}, u32[]{:S(2)}) collective-permute-start(bf16[4,96,768]{2,1,0:T(8,128)(2,1)} %get-tuple-element.6), channel_id=1, source_target_pairs={{15,0},{0,1},{1,2},{2,3},{3,4},{4,5},{5,6},{6,7},{7,8},{8,9},{9,10... | collective-permute-start | bytes 1769480 | tf_op jit(solution)/shard_map/ppermute | solution.py:287
  16.3 18.2 %collective-permute-start.1 = (bf16[4,96,768]{2,1,0:T(8,128)(2,1)}, bf16[4,96,768]{2,1,0:T(8,128)(2,1)S(1)}, u32[]{:S(2)}, u32[]{:S(2)}) collective-permute-start(bf16[4,96,768]{2,1,0:T(8,128)(2,1)} %get-tuple-element.7), channel_id=1, source_target_pairs={{1,0},{2,1},{3,2},{4,3},{5,4},{6,5},{7,6},{8,7},{9,8},{10,9},{11,1... | collective-permute-start | bytes 1769480 | tf_op jit(solution)/shard_map/ppermute | solution.py:287
  32.6 1.9 %copy-start.1 = (bf16[4,96,768]{2,1,0:T(8,128)(2,1)}, bf16[4,96,768]{2,1,0:T(8,128)(2,1)S(1)}, u32[]{:S(2)}) copy-start(bf16[4,96,768]{2,1,0:T(8,128)(2,1)S(1)} %collective-permute-done.lower_ref) | copy-start | bytes 1769476
  34.5 0.8 %copy-start.2 = (bf16[4,96,768]{2,1,0:T(8,128)(2,1)}, bf16[4,96,768]{2,1,0:T(8,128)(2,1)S(1)}, u32[]{:S(2)}) copy-start(bf16[4,96,768]{2,1,0:T(8,128)(2,1)S(1)} %collective-permute-done.1.upper_ref) | copy-start | bytes 1769476
  34.5 1.0 %copy-start = (bf16[16,152,128]{2,1,0:T(8,128)(2,1)}, bf16[16,152,128]{2,1,0:T(8,128)(2,1)S(1)}, u32[]{:S(2)}) copy-start(bf16[16,152,128]{2,1,0:T(8,128)(2,1)S(1)} %all-to-all-done) | copy-start | bytes 1867780

commit v2 on v1

v2 whole, which is shorter than its diff:
```python
import jax
import jax.numpy as jnp
from jax import lax
from jax.experimental import pallas as pl
from jax.experimental.pallas import tpu as pltpu
from jax.sharding import PartitionSpec as P


HEAD = 96
MIG = 4
EPSILON = 1e-05
LANES = 128
TILE = 8
FOLD = 2

BF16 = jnp.bfloat16
F32 = jnp.float32
I32 = jnp.int32


def iota(shape, axis):
    return lax.broadcasted_iota(I32, shape, axis)


def ones_where(condition):
    return jnp.where(condition, 1.0, 0.0).astype(BF16)


def matmul(left, right):
    return jnp.dot(left, right, preferred_element_type=F32)


def matmul_nt(left, right):
    return lax.dot_general(left, right, (((1,), (1,)), ((), ())), preferred_element_type=F32)


def in_vmem(array):
    return pltpu.with_memory_space_constraint(array, pltpu.VMEM)


def in_hbm(array):
    return pltpu.with_memory_space_constraint(array, pltpu.HBM)


def round_up(value, multiple):
    return -(-value // multiple) * multiple


def whole(*spaces):
    return [pl.BlockSpec(memory_space=space) for space in spaces]


def block_sizes(width, capacity):
    slots = round_up(capacity, TILE // FOLD)
    group_rows = FOLD * slots
    groups = width // FOLD // LANES
    return slots, group_rows, groups, groups * group_rows + TILE


def pack_frames(frames, route_peer, route_pos, peers, capacity):
    row_count, width = frames.shape
    slots, group_rows, groups, block_rows = block_sizes(width, capacity)
    half = width // FOLD

    def body(frames_ref, peer_ref, pos_ref, out_ref):
        peer = peer_ref[...]
        owner = ones_where(iota((peers, row_count), 0) == peer)
        earlier = ones_where(iota((row_count, row_count), 0) < iota((row_count, row_count), 1))
        running = matmul(owner, earlier)
        slot = jnp.sum(running * owner.astype(F32), axis=0, keepdims=True).astype(I32)
        flat = peer * group_rows + slot
        rows = iota((peers * group_rows, row_count), 0)
        pick = jnp.concatenate([ones_where(rows == flat + h * slots) for h in range(FOLD)], axis=1)
        source = jnp.concatenate(
            [frames_ref[:, h * half : (h + 1) * half] for h in range(FOLD)], axis=0
        )
        packed = matmul(pick, source).astype(BF16)
        owner_tile = ones_where(iota((peers * TILE, row_count), 0) // TILE == peer)
        lane = iota((LANES, row_count), 0)
        in_lane = (lane % slots == slot) & (lane < group_rows)
        code = jnp.where(in_lane, (pos_ref[...] + 1).astype(F32), 0.0).astype(BF16)
        codes = matmul_nt(owner_tile, code).astype(BF16)
        for p in range(peers):
            for g in range(groups):
                out_ref[p * block_rows + g * group_rows : p * block_rows + (g + 1) * group_rows, :] = (
                    packed[p * group_rows : (p + 1) * group_rows, g * LANES : (g + 1) * LANES]
                )
            out_ref[(p + 1) * block_rows - TILE : (p + 1) * block_rows, :] = codes[
                p * TILE : (p + 1) * TILE, :
            ]

    return pl.pallas_call(
        body,
        out_shape=jax.ShapeDtypeStruct((peers * block_rows, LANES), BF16),
        in_specs=whole(pltpu.VMEM, pltpu.VMEM, pltpu.VMEM),
        out_specs=pl.BlockSpec(memory_space=pltpu.VMEM),
        compiler_params=pltpu.CompilerParams(vmem_limit_bytes=12 << 20),
        name="pack_frames",
    )(in_hbm(frames), in_hbm(route_peer.reshape(1, -1)), in_hbm(route_pos.reshape(1, -1)))


def pack_streams(destination, key_cache, value_cache, conv_state, peers):
    streams, left, width = key_cache.shape
    tail = conv_state.shape[0]
    rows = 2 * left + 1 + tail

    def body(dest_ref, own_ref, key_ref, value_ref, conv_ref, up_ref, down_ref, conv_f32):
        own = own_ref[0]
        conv_f32[...] = conv_ref[...].astype(F32)
        up_ref[...] = jnp.zeros_like(up_ref)
        down_ref[...] = jnp.zeros_like(down_ref)

        def put(out_ref, rank, j, slot):
            out_ref[rank, 0:left, :] = key_ref[j]
            out_ref[rank, left : 2 * left, :] = value_ref[j]
            code = jnp.full((1, width), slot + 1, I32).astype(F32)
            out_ref[rank, 2 * left : rows, :] = jnp.concatenate(
                [code, conv_f32[:, j, :]], axis=0
            ).astype(BF16)

        def step(chosen_device, out_ref):
            rank = jnp.int32(0)
            for j in range(streams):
                target = dest_ref[j]
                chosen = target // streams == chosen_device

                @pl.when(chosen)
                def _():
                    put(out_ref, jnp.minimum(rank, MIG - 1), j, target % streams)

                rank = rank + chosen.astype(I32)

        step((own + 1) % peers, up_ref)
        step((own + peers - 1) % peers, down_ref)

    bundle = jax.ShapeDtypeStruct((MIG, rows, width), BF16)
    return pl.pallas_call(
        body,
        out_shape=(bundle, bundle),
        in_specs=whole(pltpu.SMEM, pltpu.SMEM, pltpu.VMEM, pltpu.VMEM, pltpu.VMEM),
        out_specs=whole(pltpu.VMEM, pltpu.VMEM),
        scratch_shapes=[pltpu.VMEM((tail, streams, width), F32)],
        compiler_params=pltpu.CompilerParams(vmem_limit_bytes=12 << 20),
        name="pack_streams",
    )(*map(in_hbm, (destination, own_index(), key_cache, value_cache, conv_state)))


def own_index():
    return lax.axis_index("streams").astype(I32).reshape(1)


def settle_streams(
    from_lower, from_upper, destination, valid_count, key_cache, value_cache, conv_state,
    qkv_weight, conv_kernel, span,
):
    streams, left, width = key_cache.shape
    tail = conv_state.shape[0]
    taps = conv_kernel.shape[0]
    model = qkv_weight.shape[0]

    def body(
        dest_ref, own_ref, valid_ref, lower_ref, upper_ref, key_ref, value_ref, conv_ref, taps_ref,
        weight_hbm, keys_old, values_old, keys_next, values_next, conv_next, conv_part, weight_ref,
        conv_in, conv_f32, taps_f32, sem,
    ):
        weight_copy = pltpu.make_async_copy(weight_hbm.at[:, 0:width], weight_ref, sem)
        weight_copy.start()
        own = own_ref[0]
        codes = [
            (bundle_ref, j, jnp.max(bundle_ref[j, 2 * left : 2 * left + 1, :].astype(F32)).astype(I32))
            for bundle_ref in (lower_ref, upper_ref)
            for j in range(MIG)
        ]
        taps_f32[...] = taps_ref[...].astype(F32)
        conv_f32[...] = conv_ref[...].astype(F32)
        for j in range(streams):
            target = dest_ref[j]

            @pl.when(target // streams == own)
            def _():
                slot = target % streams
                keys_old[slot] = key_ref[j]
                values_old[slot] = value_ref[j]
                conv_in[slot, 1 : 1 + tail, :] = conv_f32[:, j, :]

        for bundle_ref, j, code in codes:

            @pl.when(code > 0)
            def _():
                keys_old[code - 1] = bundle_ref[j, 0:left, :]
                values_old[code - 1] = bundle_ref[j, left : 2 * left, :]
                conv_in[code - 1] = bundle_ref[j, 2 * left : 2 * left + 1 + tail, :].astype(F32)

        conv_in[:, 0:1, :] = jnp.zeros((streams, 1, width), F32)
        pick_row = iota((left, left), 0)
        pick_col = iota((left, left), 1)
        conv_row = iota((tail, 1 + tail), 0)
        conv_col = iota((tail, 1 + tail), 1)
        for s in range(streams):
            valid = valid_ref[s]
            pick = ones_where(pick_col == pick_row + valid)
            keys_next[s] = matmul(pick, keys_old[s]).astype(BF16)
            values_next[s] = matmul(pick, values_old[s]).astype(BF16)
            conv_pick = ones_where(conv_col == conv_row + (valid + 1))
            conv_f32[:, s, :] = matmul(conv_pick, conv_in[s].astype(BF16))
        conv_next[...] = conv_f32[...].astype(BF16)
        for c in range(width // LANES):
            lanes = slice(c * LANES, (c + 1) * LANES)
            inputs = [conv_in[:, 1 + j, lanes] for j in range(tail)]
            for t in range(span):
                total = jnp.zeros((streams, LANES), F32)
                for i in range(min(taps, tail - t)):
                    total = total + taps_f32[i : i + 1, lanes] * inputs[t + i]
                conv_part[t, :, lanes] = total
        weight_copy.wait()

    cache = pltpu.HBM(key_cache.shape, BF16)
    return pl.pallas_call(
        body,
        out_shape=(
            cache, cache, cache, cache,
            pltpu.HBM(conv_state.shape, BF16),
            pltpu.HBM((span, streams, width), F32),
            pltpu.VMEM((model, width), BF16),
        ),
        in_specs=whole(*[pltpu.SMEM] * 3, *[pltpu.VMEM] * 6, pl.ANY),
        out_specs=whole(*[pltpu.VMEM] * 7),
        scratch_shapes=[
            pltpu.VMEM((streams, 1 + tail, width), F32),
            pltpu.VMEM((tail, streams, width), F32),
            pltpu.VMEM((taps, width), F32),
            pltpu.SemaphoreType.DMA,
        ],
        compiler_params=pltpu.CompilerParams(vmem_limit_bytes=24 << 20),
        name="settle_streams",
    )(
        *map(
            in_hbm,
            (
                destination, own_index(), valid_count, from_lower, from_upper, key_cache,
                value_cache, conv_state, conv_kernel, qkv_weight,
            ),
        )
    )


def stream_step(received, valid_count, settled, qkv_weight, conv_kernel, peers, row_count, capacity):
    keys_old, values_old, keys_kept, values_kept, conv_kept, conv_part, first_weight = settled
    streams, left, width = keys_old.shape
    tail = conv_kept.shape[0]
    taps = conv_kernel.shape[0]
    span = row_count // streams
    model = qkv_weight.shape[0]
    half = model // FOLD
    heads = width // HEAD
    keys = left + span
    slots, group_rows, groups, block_rows = block_sizes(model, capacity)
    packed_rows = peers * group_rows

    def body(
        valid_ref, recv_ref, first_ref, key_hbm, value_hbm, keys_kept_hbm, values_kept_hbm,
        conv_kept_hbm, conv_part_hbm, weight_hbm, taps_hbm, encoded_hbm, keys_next_hbm,
        values_next_hbm, conv_next_hbm,
        keys_all, values_all, keys_kept_ref, values_kept_ref, conv_kept_ref, conv_part_ref,
        weight_ref, taps_ref, encoded_ref, keys_next_ref, values_next_ref, conv_next_ref,
        gathered, attended_all, attended_f32, taps_f32, encoded_f32, in_sems, weight_sems, out_sems,
    ):
        weight_copies = [
            pltpu.make_async_copy(
                weight_hbm.at[:, (c + 1) * width : (c + 2) * width],
                weight_ref.at[c],
                weight_sems.at[c],
            )
            for c in range(2)
        ]
        in_copies = [
            pltpu.make_async_copy(source, target, in_sems.at[n])
            for n, (source, target) in enumerate(
                (
                    (key_hbm, keys_all.at[:, 0:left, :]),
                    (value_hbm, values_all.at[:, 0:left, :]),
                    (keys_kept_hbm, keys_kept_ref),
                    (values_kept_hbm, values_kept_ref),
                    (conv_kept_hbm, conv_kept_ref),
                    (conv_part_hbm, conv_part_ref),
                    (taps_hbm, taps_ref),
                )
            )
        ]
        out_copies = [
            pltpu.make_async_copy(source, target, out_sems.at[n])
            for n, (source, target) in enumerate(
                (
                    (encoded_ref, encoded_hbm), (keys_next_ref, keys_next_hbm),
                    (values_next_ref, values_next_hbm), (conv_next_ref, conv_next_hbm),
                )
            )
        ]
        for copy in weight_copies + in_copies:
            copy.start()

        for p in range(peers):
            for g in range(groups):
                gathered[p * group_rows : (p + 1) * group_rows, g * LANES : (g + 1) * LANES] = recv_ref[
                    p * block_rows + g * group_rows : p * block_rows + (g + 1) * group_rows, :
                ]
        codes = jnp.concatenate(
            [recv_ref[(p + 1) * block_rows - TILE : (p + 1) * block_rows, :] for p in range(peers)],
            axis=0,
        )
        spread_lane = ones_where(
            iota((LANES, packed_rows), 1) % group_rows == iota((LANES, packed_rows), 0)
        )
        spread = matmul(codes, spread_lane)
        column = iota((peers * TILE, packed_rows), 1)
        own_tile = iota((peers * TILE, packed_rows), 0) == column // group_rows * TILE
        position = jnp.sum(jnp.where(own_tile, spread, 0.0), axis=0, keepdims=True).astype(I32)
        out_row = iota((row_count, packed_rows), 0) + 1
        column_half = iota((row_count, packed_rows), 1) % group_rows // slots
        hit = out_row == position
        place = jnp.concatenate([ones_where(hit & (column_half == h)) for h in range(FOLD)], axis=0)
        halves = matmul(place, gathered[...])
        owned = jnp.concatenate(
            [halves[h * row_count : (h + 1) * row_count, :] for h in range(FOLD)], axis=1
        )
        centered = owned - jnp.mean(owned, axis=-1, keepdims=True)
        spread_of = jnp.mean(centered * centered, axis=-1, keepdims=True)
        normed = (centered * lax.rsqrt(spread_of + EPSILON)).astype(BF16)
        queries_new = matmul(normed, first_ref[...]).astype(BF16)
        weight_copies[0].wait()
        keys_new = matmul(normed, weight_ref[0]).astype(BF16)
        weight_copies[1].wait()
        values_new = matmul(normed, weight_ref[1]).astype(BF16)
        for copy in in_copies:
            copy.wait()

        def new_rows(row_stream, row_index, kept):
            column = iota(row_stream.shape, 1)
            valid = jnp.zeros(row_stream.shape, I32)
            for s in range(streams):
                valid = jnp.where(row_stream == s, valid_ref[s], valid)
            frame = row_index + valid - kept
            return ones_where((frame >= 0) & (column == row_stream * span + frame))

        row = iota((streams * left, row_count), 0)
        cache_pick = new_rows(row // left, row % left, left)
        cache_shape = (streams, left, width)
        keys_next_ref[...] = (
            keys_kept_ref[...].astype(F32) + matmul(cache_pick, keys_new).reshape(cache_shape)
        ).astype(BF16)
        values_next_ref[...] = (
            values_kept_ref[...].astype(F32) + matmul(cache_pick, values_new).reshape(cache_shape)
        ).astype(BF16)
        out_copies[1].start()
        out_copies[2].start()

        head_rows = heads * span
        head_mask = ones_where(
            iota((head_rows, width), 1) // HEAD == iota((head_rows, width), 0) // span
        )
        t_of = iota((keys, head_rows), 1) % span
        key_of = iota((keys, head_rows), 0) - left
        t_row = iota((span, width), 0)
        lane_head = iota((span, width), 1) // HEAD
        for s in range(streams):
            valid = valid_ref[s]
            rows = slice(s * span, (s + 1) * span)
            keys_all[s, left:keys, :] = keys_new[rows, :]
            values_all[s, left:keys, :] = values_new[rows, :]
            queries = jnp.concatenate([queries_new[rows, :]] * heads, axis=0) * head_mask
            scores = matmul_nt(keys_all[s], queries) * HEAD ** (-0.5)
            allowed = (key_of < 0) | ((key_of <= t_of) & (key_of < valid))
            scores = jnp.where(allowed, scores, -1e30)
            weights = jnp.exp(scores - jnp.max(scores, axis=0, keepdims=True))
            probabilities = (weights / jnp.sum(weights, axis=0, keepdims=True)).astype(BF16)
            mixed = lax.dot_general(
                probabilities, values_all[s], (((0,), (0,)), ((), ())), preferred_element_type=F32
            )
            attended = mixed[0:span, :]
            for h in range(1, heads):
                attended = jnp.where(lane_head == h, mixed[h * span : (h + 1) * span, :], attended)
            attended = jnp.where(t_row < valid, attended, 0.0).astype(BF16)
            attended_all[rows, :] = attended
            attended_f32[s] = attended.astype(F32)

        row = iota((tail * streams, row_count), 0)
        conv_pick = new_rows(row % streams, row // streams, tail)
        conv_next_ref[...] = (
            conv_kept_ref[...].astype(F32)
            + matmul(conv_pick, attended_all[...]).reshape(tail, streams, width)
        ).astype(BF16)
        out_copies[3].start()

        taps_f32[...] = taps_ref[...].astype(F32)
        stream_of = iota((streams, LANES), 0)
        valid_rows = jnp.zeros((streams, LANES), I32)
        for s in range(streams):
            valid_rows = jnp.where(stream_of == s, valid_ref[s], valid_rows)
        for c in range(width // LANES):
            lanes = slice(c * LANES, (c + 1) * LANES)
            inputs = [attended_f32[:, t, lanes] for t in range(span)]
            for t in range(span):
                total = conv_part_ref[t, :, lanes] + inputs[t]
                for i in range(max(tail - t, 0), taps):
                    total = total + taps_f32[i : i + 1, lanes] * inputs[t + i - tail]
                encoded_f32[:, t, lanes] = jnp.where(t < valid_rows, total, 0.0)
        encoded_ref[...] = encoded_f32[...].reshape(row_count, width).astype(BF16)
        out_copies[0].start()
        for copy in out_copies:
            copy.wait()

    encoded_shape = (row_count, width)
    cache_shape = (streams, left, width)
    conv_shape = (tail, streams, width)
    out_shapes = (encoded_shape, cache_shape, cache_shape, conv_shape)
    return pl.pallas_call(
        body,
        out_shape=[jax.ShapeDtypeStruct(shape, BF16) for shape in out_shapes],
        in_specs=whole(pltpu.SMEM, *[pltpu.VMEM] * 2, *[pl.ANY] * 8),
        out_specs=whole(*[pl.ANY] * 4),
        scratch_shapes=[
            pltpu.VMEM((streams, keys, width), BF16),
            pltpu.VMEM((streams, keys, width), BF16),
            pltpu.VMEM(cache_shape, BF16),
            pltpu.VMEM(cache_shape, BF16),
            pltpu.VMEM(conv_shape, BF16),
            pltpu.VMEM((span, streams, width), F32),
            pltpu.VMEM((2, model, width), BF16),
            pltpu.VMEM((taps, width), BF16),
            *[pltpu.VMEM(shape, BF16) for shape in out_shapes],
            pltpu.VMEM((packed_rows, half), BF16),
            pltpu.VMEM((row_count, width), BF16),
            pltpu.VMEM((streams, span, width), F32),
            pltpu.VMEM((taps, width), F32),
            pltpu.VMEM((streams, span, width), F32),
            pltpu.SemaphoreType.DMA((7,)),
            pltpu.SemaphoreType.DMA((2,)),
            pltpu.SemaphoreType.DMA((4,)),
        ],
        compiler_params=pltpu.CompilerParams(vmem_limit_bytes=32 << 20),
        name="stream_step",
    )(
        in_hbm(valid_count), in_vmem(received), in_vmem(first_weight),
        *map(
            in_hbm,
            (
                keys_old, values_old, keys_kept, values_kept, conv_kept, conv_part, qkv_weight,
                conv_kernel,
            ),
        ),
    )


def from_behind(block, axis, distance):
    count = lax.axis_size(axis)
    return lax.ppermute(block, axis, [((i - distance) % count, i) for i in range(count)])


def local(
    frames, route_peer, route_pos, destination, valid_count, key_cache, value_cache, conv_state,
    qkv_weight, conv_kernel,
):
    peers = lax.axis_size("streams")
    row_count = frames.shape[0]
    per_peer = row_count // peers
    capacity = per_peer + per_peer // 2
    conv_by_time = conv_state.transpose(1, 0, 2)
    up, down = pack_streams(destination, key_cache, value_cache, conv_by_time, peers)
    from_lower = from_behind(up, "streams", 1)
    from_upper = from_behind(down, "streams", -1)
    packed = pack_frames(frames, route_peer, route_pos, peers, capacity)
    received = lax.all_to_all(packed, "streams", split_axis=0, concat_axis=0, tiled=True)
    settled = settle_streams(
        from_lower, from_upper, destination, valid_count, key_cache, value_cache,
        conv_by_time, qkv_weight, conv_kernel, row_count // key_cache.shape[0],
    )
    encoded, keys_next, values_next, conv_next = stream_step(
        received, valid_count, settled, qkv_weight, conv_kernel, peers, row_count, capacity
    )
    return encoded, keys_next, values_next, conv_next.transpose(1, 0, 2)


def solution(mesh):
    rows = P(("groups", "streams"))
    return jax.shard_map(
        local,
        mesh=mesh,
        in_specs=(rows,) * 8 + (P(), P()),
        out_specs=(rows,) * 4,
        check_vma=False,
    )
```

time: 51.7 us -> 50.1 us (0.969)
  the two profiles are of different devices: /device:TPU:1 before, /device:TPU:0 now
where the time goes in v2:
time: 50.1 us; the launch traced here: 49.8 us
  Pallas kernels  19.4 us (39%)
  waiting for transfers between devices  16.1 us (32%)
  starting transfers between devices  11.9 us (24%)
  local copies, waits for them, and re-layouts  1.65 us (3%)
  between operations  0.67 us (1%)
    ppermute x2, waiting for transfers between devices, from_behind(): lax.ppermute(block, axis, [((i - distance) % count, i) for i in range(cou...  16.1 us
    pallas_call x1, Pallas kernels, stream_step(): pl.pallas_call(body, out_shape=[jax.ShapeDtypeStruct(shape, BF16) for sha...  10.5 us
    all_to_all x1, starting transfers between devices, local(): lax.all_to_all(packed, 'streams', split_axis=0, concat_axis=0, tiled=True)  7.41 us
    pallas_call x1, Pallas kernels, settle_streams(): pl.pallas_call(body, out_shape=(cache, cache, cache, cache, pltpu.HBM(con...  4.89 us
    ppermute x2, starting transfers between devices, from_behind(): lax.ppermute(block, axis, [((i - distance) % count, i) for i in range(cou...  4.49 us
    pallas_call x1, Pallas kernels, pack_frames(): pl.pallas_call(body, out_shape=jax.ShapeDtypeStruct((peers * block_rows,...  2.29 us
    pallas_call x1, Pallas kernels, pack_streams(): pl.pallas_call(body, out_shape=(bundle, bundle), in_specs=whole(pltpu.SME...  1.72 us
    unnamed x4, local copies, waits for them, and re-layouts  1.65 us
  transfers between devices with their start and end apart: 3, of which 1 were waited for; matrix products, arithmetic and copies ran while one was open for 0% of the time, Pallas kernels for 13%

profile of v2, /device:TPU:0, one launch (start us, length us, event | category | flops | bytes accessed | tf_op | source)
XLA Modules:
  0.0 49.8 jit_solution(13941968571746934702)
XLA Ops:
  0.6 2.3 %pack_frames.1 = bf16[2432,128]{1,0:T(8,128)(2,1)} custom-call(bf16[128,1536]{1,0:T(8,128)(2,1)} %frames_ref.1, s32[1,128]{1,0:T(1,128)} %bitcast.10, s32[1,128]{1,0:T(1,128)} %bitcast.11), custom_call_target="tpu_custom_call" | custom-call | tf_op jit(solution)/shard_map/pack_frames/pallas_call | solution.py:92
  2.9 7.4 %all-to-all-start = ((bf16[16,152,128]{2,1,0:T(8,128)(2,1)}), bf16[16,152,128]{2,1,0:T(8,128)(2,1)S(1)}, u32[]{:S(2)}, u32[]{:S(2)}) async-start(bf16[16,152,128]{2,1,0:T(8,128)(2,1)} %bitcast.2), calls=%async_computation | async-start | bytes 1245184 | tf_op jit(solution)/shard_map/all_to_all | solution.py:472
  10.3 1.7 %pack_streams.1 = (bf16[4,96,768]{2,1,0:T(8,128)(2,1)S(1)}, bf16[4,96,768]{2,1,0:T(8,128)(2,1)S(1)}) custom-call(s32[8]{0:T(128)} %dest_ref.3, s32[1]{0:T(128)} %bitcast.4.own_ref, bf16[8,32,768]{2,1,0:T(8,128)(2,1)} %key_ref.3, bf16[8,32,768]{2,1,0:T(8,128)(2,1)} %value_ref.3, bf16[31,8,768]{2,1,0:T(8,128)(2,1)} %bitcast.8), custom_call_target="tpu_custom_call" | custom-call | tf_op jit(solution)/shard_map/pack_streams/pallas_call | solution.py:137
  12.1 0.5 collective-permute-start
  12.5 4.0 %collective-permute-start.1 = (bf16[4,96,768]{2,1,0:T(8,128)(2,1)S(1)}, bf16[4,96,768]{2,1,0:T(8,128)(2,1)S(1)}, u32[]{:S(2)}, u32[]{:S(2)}) collective-permute-start(bf16[4,96,768]{2,1,0:T(8,128)(2,1)S(1)} %get-tuple-element.18), channel_id=1, source_target_pairs={{1,0},{2,1},{3,2},{4,3},{5,4},{6,5},{7,6},{8,7},{9,8},{10,9},{11,1... | collective-permute-start | bytes 1769480 | tf_op jit(solution)/shard_map/ppermute | solution.py:456
  16.6 16.1 %collective-permute-done.lower_ref = bf16[4,96,768]{2,1,0:T(8,128)(2,1)S(1)} collective-permute-done((bf16[4,96,768]{2,1,0:T(8,128)(2,1)S(1)}, bf16[4,96,768]{2,1,0:T(8,128)(2,1)S(1)}, u32[]{:S(2)}, u32[]{:S(2)}) %collective-permute-start) | collective-permute-done | bytes 589856 | tf_op jit(solution)/shard_map/ppermute | solution.py:456
  32.7 0.0 copy-start
  32.7 0.0 collective-permute-done.1.upper_ref
  32.7 0.8 %copy-done = bf16[4,96,768]{2,1,0:T(8,128)(2,1)} copy-done((bf16[4,96,768]{2,1,0:T(8,128)(2,1)}, bf16[4,96,768]{2,1,0:T(8,128)(2,1)S(1)}, u32[]{:S(2)}) %copy-start) | copy-done | bytes 589848
  33.5 0.0 copy-start.1
  33.5 0.8 %copy-done.1 = bf16[4,96,768]{2,1,0:T(8,128)(2,1)} copy-done((bf16[4,96,768]{2,1,0:T(8,128)(2,1)}, bf16[4,96,768]{2,1,0:T(8,128)(2,1)S(1)}, u32[]{:S(2)}) %copy-start.1) | copy-done | bytes 589848
  34.4 4.9 %settle_streams.1 = (bf16[8,32,768]{2,1,0:T(8,128)(2,1)}, bf16[8,32,768]{2,1,0:T(8,128)(2,1)}, bf16[8,32,768]{2,1,0:T(8,128)(2,1)}, bf16[8,32,768]{2,1,0:T(8,128...) custom-call(s32[8]{0:T(128)} %dest_ref.3, s32[1]{0:T(128)} %bitcast.4.own_ref, ...), custom_call_target="tpu_custom_call" | custom-call | tf_op jit(solution)/shard_map/settle_streams/pallas_call | solution.py:218
  39.3 0.0 all-to-all-done
  39.3 10.5 %stream_step.1 = (bf16[128,768]{1,0:T(8,128)(2,1)}, bf16[8,32,768]{2,1,0:T(8,128)(2,1)}, bf16[8,32,768]{2,1,0:T(8,128)(2,1)}, bf16[31,8,768]{2,1,0:T(8,128)(2,1)}) custom-call(s32[8]{0:T(128)} %valid_ref.3, bf16[2432,128]{1,0:T(8,128)(2,1)S(1)} %bitcast.7, bf16[1536,768]{1,0:T(8,128)(2,1)S(1)} %get-tuple-element.19.first_ref, ...), custom_call_target="tpu_custom_call" | custom-call | tf_op jit(solution)/shard_map/stream_step/pallas_call | solution.py:416
Async XLA Ops:
  2.9 36.3 %all-to-all-start = ((bf16[16,152,128]{2,1,0:T(8,128)(2,1)}), bf16[16,152,128]{2,1,0:T(8,128)(2,1)S(1)}, u32[]{:S(2)}, u32[]{:S(2)}) async-start(bf16[16,152,128]{2,1,0:T(8,128)(2,1)} %bitcast.2), calls=%async_computation | async-start | bytes 1245184 | tf_op jit(solution)/shard_map/all_to_all | solution.py:472
  12.1 20.6 %collective-permute-start = (bf16[4,96,768]{2,1,0:T(8,128)(2,1)S(1)}, bf16[4,96,768]{2,1,0:T(8,128)(2,1)S(1)}, u32[]{:S(2)}, u32[]{:S(2)}) collective-permute-start(bf16[4,96,768]{2,1,0:T(8,128)(2,1)S(1)} %get-tuple-element.17), channel_id=1, source_target_pairs={{15,0},{0,1},{1,2},{2,3},{3,4},{4,5},{5,6},{6,7},{7,8},{8,9},{9,10... | collective-permute-start | bytes 1769480 | tf_op jit(solution)/shard_map/ppermute | solution.py:456
  12.5 20.2 %collective-permute-start.1 = (bf16[4,96,768]{2,1,0:T(8,128)(2,1)S(1)}, bf16[4,96,768]{2,1,0:T(8,128)(2,1)S(1)}, u32[]{:S(2)}, u32[]{:S(2)}) collective-permute-start(bf16[4,96,768]{2,1,0:T(8,128)(2,1)S(1)} %get-tuple-element.18), channel_id=1, source_target_pairs={{1,0},{2,1},{3,2},{4,3},{5,4},{6,5},{7,6},{8,7},{9,8},{10,9},{11,1... | collective-permute-start | bytes 1769480 | tf_op jit(solution)/shard_map/ppermute | solution.py:456
  32.7 0.8 %copy-start = (bf16[4,96,768]{2,1,0:T(8,128)(2,1)}, bf16[4,96,768]{2,1,0:T(8,128)(2,1)S(1)}, u32[]{:S(2)}) copy-start(bf16[4,96,768]{2,1,0:T(8,128)(2,1)S(1)} %collective-permute-done.lower_ref) | copy-start | bytes 1769476
  33.5 0.8 %copy-start.1 = (bf16[4,96,768]{2,1,0:T(8,128)(2,1)}, bf16[4,96,768]{2,1,0:T(8,128)(2,1)S(1)}, u32[]{:S(2)}) copy-start(bf16[4,96,768]{2,1,0:T(8,128)(2,1)S(1)} %collective-permute-done.1.upper_ref) | copy-start | bytes 1769476

commit v3 on v1

v3 whole, which is shorter than its diff:
```python
import jax
import jax.numpy as jnp
from jax import lax
from jax.experimental import pallas as pl
from jax.experimental.pallas import tpu as pltpu
from jax.sharding import PartitionSpec as P


HEAD = 96
MIG = 4
EPSILON = 1e-05
LANES = 128
TILE = 8
FOLD = 2
CHUNKS = 3

BF16 = jnp.bfloat16
F32 = jnp.float32
I32 = jnp.int32


def iota(shape, axis):
    return lax.broadcasted_iota(I32, shape, axis)


def ones_where(condition):
    return jnp.where(condition, 1.0, 0.0).astype(BF16)


def matmul(left, right):
    return jnp.dot(left, right, preferred_element_type=F32)


def matmul_nt(left, right):
    return lax.dot_general(left, right, (((1,), (1,)), ((), ())), preferred_element_type=F32)


def in_vmem(array):
    return pltpu.with_memory_space_constraint(array, pltpu.VMEM)


def in_hbm(array):
    return pltpu.with_memory_space_constraint(array, pltpu.HBM)


def round_up(value, multiple):
    return -(-value // multiple) * multiple


def whole(*spaces):
    return [pl.BlockSpec(memory_space=space) for space in spaces]


def block_sizes(width, capacity):
    slots = round_up(capacity, TILE // FOLD)
    group_rows = FOLD * slots
    groups = width // FOLD // LANES
    return slots, group_rows, groups, groups * group_rows + TILE


def pack_all(
    frames, route_peer, route_pos, destination, key_cache, value_cache, conv_state, peers, capacity
):
    row_count, model = frames.shape
    slots, group_rows, groups, block_rows = block_sizes(model, capacity)
    half = model // FOLD
    streams, left, width = key_cache.shape
    tail = conv_state.shape[0]
    rows = 2 * left + 1 + tail

    def body(
        dest_ref, own_ref, peer_ref, pos_ref, key_hbm, value_hbm, conv_hbm, frames_hbm,
        packed_ref, up_ref, down_ref, key_ref, value_ref, conv_ref, frames_ref, conv_f32, sems,
    ):
        copies = [
            pltpu.make_async_copy(source, target, sems.at[n])
            for n, (source, target) in enumerate(
                (
                    (frames_hbm, frames_ref), (conv_hbm, conv_ref), (key_hbm, key_ref),
                    (value_hbm, value_ref),
                )
            )
        ]
        for copy in copies:
            copy.start()
        own = own_ref[0]
        peer = peer_ref[...]
        owner = ones_where(iota((peers, row_count), 0) == peer)
        earlier = ones_where(iota((row_count, row_count), 0) < iota((row_count, row_count), 1))
        running = matmul(owner, earlier)
        slot = jnp.sum(running * owner.astype(F32), axis=0, keepdims=True).astype(I32)
        flat = peer * group_rows + slot
        packed_row = iota((peers * group_rows, row_count), 0)
        pick = jnp.concatenate(
            [ones_where(packed_row == flat + h * slots) for h in range(FOLD)], axis=1
        )
        owner_tile = ones_where(iota((peers * TILE, row_count), 0) // TILE == peer)
        lane = iota((LANES, row_count), 0)
        in_lane = (lane % slots == slot) & (lane < group_rows)
        code = jnp.where(in_lane, (pos_ref[...] + 1).astype(F32), 0.0).astype(BF16)
        codes = matmul_nt(owner_tile, code).astype(BF16)
        copies[0].wait()
        source = jnp.concatenate(
            [frames_ref[:, h * half : (h + 1) * half] for h in range(FOLD)], axis=0
        )
        packed = matmul(pick, source).astype(BF16)
        for p in range(peers):
            for g in range(groups):
                first = p * block_rows + g * group_rows
                packed_ref[first : first + group_rows, :] = packed[
                    p * group_rows : (p + 1) * group_rows, g * LANES : (g + 1) * LANES
                ]
            packed_ref[(p + 1) * block_rows - TILE : (p + 1) * block_rows, :] = codes[
                p * TILE : (p + 1) * TILE, :
            ]
        copies[1].wait()
        conv_f32[...] = conv_ref[...].astype(F32)
        copies[2].wait()
        copies[3].wait()

        def put(out_ref, rank, j, slot):
            out_ref[rank, 0:left, :] = key_ref[j]
            out_ref[rank, left : 2 * left, :] = value_ref[j]
            code = jnp.full((1, width), slot + 1, I32).astype(F32)
            out_ref[rank, 2 * left : rows, :] = jnp.concatenate(
                [code, conv_f32[:, j, :]], axis=0
            ).astype(BF16)

        for out_ref, chosen_device in (
            (up_ref, (own + 1) % peers), (down_ref, (own + peers - 1) % peers),
        ):
            out_ref[:, 2 * left : rows, :] = jnp.zeros((MIG, 1 + tail, width), BF16)
            rank = jnp.int32(0)
            for j in range(streams):
                target = dest_ref[j]
                chosen = target // streams == chosen_device

                @pl.when(chosen)
                def _():
                    put(out_ref, jnp.minimum(rank, MIG - 1), j, target % streams)

                rank = rank + chosen.astype(I32)

    bundle = pltpu.VMEM((MIG, rows, width), BF16)
    return pl.pallas_call(
        body,
        out_shape=(pltpu.VMEM((peers * block_rows, LANES), BF16), bundle, bundle),
        in_specs=whole(*[pltpu.SMEM] * 2, *[pltpu.VMEM] * 2, *[pl.ANY] * 4),
        out_specs=whole(*[pltpu.VMEM] * 3),
        scratch_shapes=[
            pltpu.VMEM(key_cache.shape, BF16),
            pltpu.VMEM(key_cache.shape, BF16),
            pltpu.VMEM(conv_state.shape, BF16),
            pltpu.VMEM(frames.shape, BF16),
            pltpu.VMEM(conv_state.shape, F32),
            pltpu.SemaphoreType.DMA((4,)),
        ],
        compiler_params=pltpu.CompilerParams(vmem_limit_bytes=12 << 20),
        name="pack_all",
    )(
        *map(
            in_hbm,
            (
                destination, own_index(), route_peer.reshape(1, -1), route_pos.reshape(1, -1),
                key_cache, value_cache, conv_state, frames,
            ),
        )
    )


def own_index():
    return lax.axis_index("streams").astype(I32).reshape(1)


def settle_streams(
    from_lower, from_upper, destination, key_cache, value_cache, conv_state, conv_kernel
):
    streams, left, width = key_cache.shape
    tail = conv_state.shape[0]
    cache = (streams, left, width)

    def body(
        dest_ref, own_ref, lower_ref, upper_ref, key_hbm, value_hbm, conv_hbm, taps_hbm,
        keys_old, values_old, conv_old, taps_f32,
        key_ref, value_ref, conv_ref, taps_ref, conv_f32, sems,
    ):
        copies = [
            pltpu.make_async_copy(source, target, sems.at[n])
            for n, (source, target) in enumerate(
                (
                    (conv_hbm, conv_ref), (key_hbm, key_ref), (value_hbm, value_ref),
                    (taps_hbm, taps_ref),
                )
            )
        ]
        for copy in copies:
            copy.start()
        own = own_ref[0]
        codes = [
            (bundle_ref, j, jnp.max(bundle_ref[j, 2 * left : 2 * left + 1, :].astype(F32)).astype(I32))
            for bundle_ref in (lower_ref, upper_ref)
            for j in range(MIG)
        ]
        for bundle_ref, j, code in codes:

            @pl.when(code > 0)
            def _():
                keys_old[code - 1] = bundle_ref[j, 0:left, :]
                values_old[code - 1] = bundle_ref[j, left : 2 * left, :]
                conv_old[code - 1] = bundle_ref[j, 2 * left : 2 * left + 1 + tail, :].astype(F32)

        for copy in copies:
            copy.wait()
        taps_f32[...] = taps_ref[...].astype(F32)
        conv_f32[...] = conv_ref[...].astype(F32)
        for j in range(streams):
            target = dest_ref[j]

            @pl.when(target // streams == own)
            def _():
                slot = target % streams
                keys_old[slot] = key_ref[j]
                values_old[slot] = value_ref[j]
                conv_old[slot, 1 : 1 + tail, :] = conv_f32[:, j, :]

        conv_old[:, 0:1, :] = jnp.zeros((streams, 1, width), F32)

    return pl.pallas_call(
        body,
        out_shape=(
            pltpu.VMEM(cache, BF16),
            pltpu.VMEM(cache, BF16),
            pltpu.VMEM((streams, 1 + tail, width), F32),
            pltpu.VMEM(conv_kernel.shape, F32),
        ),
        in_specs=whole(*[pltpu.SMEM] * 2, *[pltpu.VMEM] * 2, *[pl.ANY] * 4),
        out_specs=whole(*[pltpu.VMEM] * 4),
        scratch_shapes=[
            pltpu.VMEM(cache, BF16),
            pltpu.VMEM(cache, BF16),
            pltpu.VMEM(conv_state.shape, BF16),
            pltpu.VMEM(conv_kernel.shape, BF16),
            pltpu.VMEM(conv_state.shape, F32),
            pltpu.SemaphoreType.DMA((4,)),
        ],
        compiler_params=pltpu.CompilerParams(vmem_limit_bytes=16 << 20),
        name="settle_streams",
    )(
        *map(in_hbm, (destination, own_index())), in_vmem(from_lower), in_vmem(from_upper),
        *map(in_hbm, (key_cache, value_cache, conv_state, conv_kernel)),
    )


def stream_step(received, valid_count, settled, qkv_weight, peers, row_count, capacity):
    keys_settled, values_settled, conv_settled, taps_settled = settled
    streams, left, width = keys_settled.shape
    tail = conv_settled.shape[1] - 1
    taps = taps_settled.shape[0]
    span = row_count // streams
    model, columns = qkv_weight.shape
    half = model // FOLD
    chunk = columns // CHUNKS
    heads = width // HEAD
    keys = left + span
    window = 1 + tail + span
    slots, group_rows, groups, block_rows = block_sizes(model, capacity)
    packed_rows = peers * group_rows

    def body(
        valid_ref, recv_ref, keys_old, values_old, conv_old, taps_ref, weight_hbm,
        encoded_hbm, keys_next_hbm, values_next_hbm, conv_next_hbm,
        encoded_ref, keys_next_ref, values_next_ref, conv_next_ref,
        weight_ref, gathered, qkv_ref, attended_f32, conv_part, conv_f32, encoded_f32,
        weight_sems, out_sems,
    ):
        weight_copies = [
            pltpu.make_async_copy(
                weight_hbm.at[:, c * chunk : (c + 1) * chunk], weight_ref.at[c], weight_sems.at[c]
            )
            for c in range(CHUNKS)
        ]
        out_copies = [
            pltpu.make_async_copy(source, target, out_sems.at[n])
            for n, (source, target) in enumerate(
                (
                    (encoded_ref, encoded_hbm), (keys_next_ref, keys_next_hbm),
                    (values_next_ref, values_next_hbm), (conv_next_ref, conv_next_hbm),
                )
            )
        ]
        for copy in weight_copies:
            copy.start()

        for p in range(peers):
            for g in range(groups):
                gathered[p * group_rows : (p + 1) * group_rows, g * LANES : (g + 1) * LANES] = recv_ref[
                    p * block_rows + g * group_rows : p * block_rows + (g + 1) * group_rows, :
                ]
        codes = jnp.concatenate(
            [recv_ref[(p + 1) * block_rows - TILE : (p + 1) * block_rows, :] for p in range(peers)],
            axis=0,
        )
        spread_lane = ones_where(
            iota((LANES, packed_rows), 1) % group_rows == iota((LANES, packed_rows), 0)
        )
        spread = matmul(codes, spread_lane)
        column = iota((peers * TILE, packed_rows), 1)
        own_tile = iota((peers * TILE, packed_rows), 0) == column // group_rows * TILE
        position = jnp.sum(jnp.where(own_tile, spread, 0.0), axis=0, keepdims=True).astype(I32)
        out_row = iota((row_count, packed_rows), 0) + 1
        column_half = iota((row_count, packed_rows), 1) % group_rows // slots
        hit = out_row == position
        place = jnp.concatenate([ones_where(hit & (column_half == h)) for h in range(FOLD)], axis=0)
        halves = matmul(place, gathered[...])
        owned = jnp.concatenate(
            [halves[h * row_count : (h + 1) * row_count, :] for h in range(FOLD)], axis=1
        )
        centered = owned - jnp.mean(owned, axis=-1, keepdims=True)
        spread_of = jnp.mean(centered * centered, axis=-1, keepdims=True)
        normed = (centered * lax.rsqrt(spread_of + EPSILON)).astype(BF16)
        lane_chunks = [slice(c * LANES, (c + 1) * LANES) for c in range(width // LANES)]

        def old_part(lanes):
            inputs = [conv_old[:, 1 + j, lanes] for j in range(tail)]
            for t in range(span):
                total = inputs[t] * taps_ref[0:1, lanes]
                for i in range(1, min(taps, tail - t)):
                    total = total + taps_ref[i : i + 1, lanes] * inputs[t + i]
                conv_part[t, :, lanes] = total

        for c in range(CHUNKS):
            weight_copies[c].wait()
            qkv_ref[:, c * chunk : (c + 1) * chunk] = matmul(normed, weight_ref[c]).astype(BF16)
            for lanes in lane_chunks[c::CHUNKS]:
                old_part(lanes)

        head_rows = heads * span
        head_mask = ones_where(
            iota((head_rows, width), 1) // HEAD == iota((head_rows, width), 0) // span
        )
        t_of = iota((keys, head_rows), 1) % span
        key_of = iota((keys, head_rows), 0) - left
        causal = key_of <= t_of
        t_row = iota((span, LANES), 0)
        lane = iota((span, LANES), 1)
        pick_shift = iota((left, keys), 1) - iota((left, keys), 0)
        conv_shift = iota((tail, window), 1) - iota((tail, window), 0)
        all_rows = [slice(s * span, (s + 1) * span) for s in range(streams)]
        all_keys = []
        all_values = []
        all_scores = []
        for s in range(streams):
            rows = all_rows[s]
            queries = jnp.concatenate([qkv_ref[rows, 0:width]] * heads, axis=0) * head_mask
            all_keys.append(
                jnp.concatenate([keys_old[s], qkv_ref[rows, width : 2 * width]], axis=0)
            )
            all_values.append(
                jnp.concatenate([values_old[s], qkv_ref[rows, 2 * width : 3 * width]], axis=0)
            )
            all_scores.append(matmul_nt(all_keys[s], queries))
        all_probabilities = []
        for s in range(streams):
            allowed = (key_of < 0) | (causal & (key_of < valid_ref[s]))
            scores = jnp.where(allowed, all_scores[s] * HEAD ** (-0.5), -1e30)
            weights = jnp.exp(scores - jnp.max(scores, axis=0, keepdims=True))
            all_probabilities.append(
                (weights / jnp.sum(weights, axis=0, keepdims=True)).astype(BF16)
            )
        for s in range(streams):
            pick = ones_where(pick_shift == valid_ref[s])
            keys_next_ref[s] = matmul(pick, all_keys[s]).astype(BF16)
            values_next_ref[s] = matmul(pick, all_values[s]).astype(BF16)
        out_copies[1].start()
        out_copies[2].start()
        all_mixed = [
            lax.dot_general(
                all_probabilities[s], all_values[s], (((0,), (0,)), ((), ())),
                preferred_element_type=F32,
            )
            for s in range(streams)
        ]
        for s in range(streams):
            for c in range(width // LANES):
                lanes = slice(c * LANES, (c + 1) * LANES)
                first = c * LANES // HEAD
                last = ((c + 1) * LANES - 1) // HEAD
                attended = all_mixed[s][first * span : (first + 1) * span, lanes]
                for h in range(first + 1, last + 1):
                    attended = jnp.where(
                        lane >= h * HEAD - c * LANES,
                        all_mixed[s][h * span : (h + 1) * span, lanes],
                        attended,
                    )
                attended = jnp.where(t_row < valid_ref[s], attended, 0.0).astype(BF16)
                attended_f32[s, :, lanes] = attended.astype(F32)

        for s in range(streams):
            conv_pick = ones_where(conv_shift == valid_ref[s] + 1)
            conv_rows = jnp.concatenate([conv_old[s], attended_f32[s]], axis=0).astype(BF16)
            conv_f32[:, s, :] = matmul(conv_pick, conv_rows)
        conv_next_ref[...] = conv_f32[...].reshape(tail * streams, width).astype(BF16)
        out_copies[3].start()

        stream_of = iota((streams, LANES), 0)
        valid_rows = jnp.zeros((streams, LANES), I32)
        for s in range(streams):
            valid_rows = jnp.where(stream_of == s, valid_ref[s], valid_rows)
        for lanes in lane_chunks:
            inputs = [attended_f32[:, t, lanes] for t in range(span)]
            for t in range(span):
                total = conv_part[t, :, lanes] + inputs[t]
                for i in range(max(tail - t, 0), taps):
                    total = total + taps_ref[i : i + 1, lanes] * inputs[t + i - tail]
                encoded_f32[:, t, lanes] = jnp.where(t < valid_rows, total, 0.0)
        encoded_ref[...] = encoded_f32[...].reshape(row_count, width).astype(BF16)
        out_copies[0].start()
        for copy in out_copies:
            copy.wait()

    cache = (streams, left, width)
    out_shapes = ((row_count, width), cache, cache, (tail * streams, width))
    return pl.pallas_call(
        body,
        out_shape=[jax.ShapeDtypeStruct(shape, BF16) for shape in out_shapes],
        in_specs=whole(pltpu.SMEM, *[pltpu.VMEM] * 5, pl.ANY),
        out_specs=whole(*[pl.ANY] * 4),
        scratch_shapes=[
            *[pltpu.VMEM(shape, BF16) for shape in out_shapes],
            pltpu.VMEM((CHUNKS, model, chunk), BF16),
            pltpu.VMEM((packed_rows, half), BF16),
            pltpu.VMEM((row_count, columns), BF16),
            pltpu.VMEM((streams, span, width), F32),
            pltpu.VMEM((span, streams, width), F32),
            pltpu.VMEM((tail, streams, width), F32),
            pltpu.VMEM((streams, span, width), F32),
            pltpu.SemaphoreType.DMA((CHUNKS,)),
            pltpu.SemaphoreType.DMA((4,)),
        ],
        compiler_params=pltpu.CompilerParams(vmem_limit_bytes=32 << 20),
        name="stream_step",
    )(
        in_hbm(valid_count),
        *map(in_vmem, (received, keys_settled, values_settled, conv_settled, taps_settled)),
        in_hbm(qkv_weight),
    )


def from_behind(block, axis, distance):
    count = lax.axis_size(axis)
    return lax.ppermute(block, axis, [((i - distance) % count, i) for i in range(count)])


def local(
    frames, route_peer, route_pos, destination, valid_count, key_cache, value_cache, conv_state,
    qkv_weight, conv_kernel,
):
    peers = lax.axis_size("streams")
    row_count = frames.shape[0]
    per_peer = row_count // peers
    capacity = per_peer + per_peer // 2
    conv_by_time = conv_state.transpose(1, 0, 2)
    packed, up, down = pack_all(
        frames, route_peer, route_pos, destination, key_cache, value_cache, conv_by_time,
        peers, capacity,
    )
    from_lower = from_behind(up, "streams", 1)
    from_upper = from_behind(down, "streams", -1)
    received = lax.all_to_all(packed, "streams", split_axis=0, concat_axis=0, tiled=True)
    settled = settle_streams(
        from_lower, from_upper, destination, key_cache, value_cache, conv_by_time,
        conv_kernel,
    )
    encoded, keys_next, values_next, conv_next = stream_step(
        received, valid_count, settled, qkv_weight, peers, row_count, capacity
    )
    _, streams, width = conv_by_time.shape
    return (
        encoded, keys_next, values_next,
        conv_next.reshape(-1, streams, width).transpose(1, 0, 2),
    )


def solution(mesh):
    rows = P(("groups", "streams"))
    return jax.shard_map(
        local,
        mesh=mesh,
        in_specs=(rows,) * 8 + (P(), P()),
        out_specs=(rows,) * 4,
        check_vma=False,
    )
```

time: 51.7 us -> 44.1 us (0.85)
  the two profiles are of different devices: /device:TPU:1 before, /device:TPU:0 now
where the time goes in v3:
time: 44.1 us; the launch traced here: 43.8 us
  waiting for transfers between devices  17.9 us (41%)
  Pallas kernels  13.4 us (30%)
  starting transfers between devices  11.9 us (27%)
  between operations  0.67 us (2%)
    ppermute x2, waiting for transfers between devices, from_behind(): lax.ppermute(block, axis, [((i - distance) % count, i) for i in range(cou...  17.9 us
    pallas_call x1, Pallas kernels, stream_step(): pl.pallas_call(body, out_shape=[jax.ShapeDtypeStruct(shape, BF16) for sha...  7.84 us
    all_to_all x1, starting transfers between devices, local(): lax.all_to_all(packed, 'streams', split_axis=0, concat_axis=0, tiled=True)  7.42 us
    ppermute x2, starting transfers between devices, from_behind(): lax.ppermute(block, axis, [((i - distance) % count, i) for i in range(cou...  4.49 us
    pallas_call x1, Pallas kernels, pack_all(): pl.pallas_call(body, out_shape=(pltpu.VMEM((peers * block_rows, LANES), B...  3.31 us
    pallas_call x1, Pallas kernels, settle_streams(): pl.pallas_call(body, out_shape=(pltpu.VMEM(cache, BF16), pltpu.VMEM(cache...  2.23 us
  transfers between devices with their start and end apart: 3, of which 1 were waited for; matrix products, arithmetic and copies ran while one was open for 0% of the time, Pallas kernels for 5%

profile of v3, /device:TPU:0, one launch (start us, length us, event | category | flops | bytes accessed | tf_op | source)
XLA Modules:
  0.0 43.8 jit_solution(9876327731501340725)
XLA Ops:
  0.6 3.3 %pack_all.1 = (bf16[2432,128]{1,0:T(8,128)(2,1)}, bf16[4,96,768]{2,1,0:T(8,128)(2,1)S(1)}, bf16[4,96,768]{2,1,0:T(8,128)(2,1)S(1)}) custom-call(s32[8]{0:T(128)} %dest_ref.3, s32[1]{0:T(128)} %bitcast.own_ref, s32[1,128]{1,0:T(1,128)} %bitcast.12, s32[1,128]{1,0:T(1,128)} %bitcast.13, bf16[8,32,768]{2,1,0:T(8,128)(2,1)} %key_hbm.3, ...), custom_call_target="tpu_custom_call" | custom-call | tf_op jit(solution)/shard_map/pack_all/pallas_call | solution.py:145
  4.0 7.4 %all-to-all-start = ((bf16[16,152,128]{2,1,0:T(8,128)(2,1)}), bf16[16,152,128]{2,1,0:T(8,128)(2,1)S(1)}, u32[]{:S(2)}, u32[]{:S(2)}) async-start(bf16[16,152,128]{2,1,0:T(8,128)(2,1)} %bitcast.4), calls=%async_computation | async-start | bytes 1245184 | tf_op jit(solution)/shard_map/all_to_all | solution.py:469
  11.4 0.4 collective-permute-start
  11.8 4.1 %collective-permute-start.1 = (bf16[4,96,768]{2,1,0:T(8,128)(2,1)S(1)}, bf16[4,96,768]{2,1,0:T(8,128)(2,1)S(1)}, u32[]{:S(2)}, u32[]{:S(2)}) collective-permute-start(bf16[4,96,768]{2,1,0:T(8,128)(2,1)S(1)} %get-tuple-element.17), channel_id=1, source_target_pairs={{1,0},{2,1},{3,2},{4,3},{5,4},{6,5},{7,6},{8,7},{9,8},{10,9},{11,1... | collective-permute-start | bytes 1769480 | tf_op jit(solution)/shard_map/ppermute | solution.py:451
  15.9 17.9 %collective-permute-done.lower_ref = bf16[4,96,768]{2,1,0:T(8,128)(2,1)S(1)} collective-permute-done((bf16[4,96,768]{2,1,0:T(8,128)(2,1)S(1)}, bf16[4,96,768]{2,1,0:T(8,128)(2,1)S(1)}, u32[]{:S(2)}, u32[]{:S(2)}) %collective-permute-start) | collective-permute-done | bytes 589856 | tf_op jit(solution)/shard_map/ppermute | solution.py:451
  33.7 0.0 collective-permute-done.1.upper_ref
  33.8 2.2 %settle_streams.1 = (bf16[8,32,768]{2,1,0:T(8,128)(2,1)S(1)}, bf16[8,32,768]{2,1,0:T(8,128)(2,1)S(1)}, f32[8,32,768]{2,1,0:T(8,128)S(1)}, f32[32,768]{1,0:T(8,128)S(1)}) custom-call(s32[8]{0:T(128)} %dest_ref.3, s32[1]{0:T(128)} %bitcast.own_ref, bf16[4,96,768]{2,1,0:T(8,128)(2,1)S(1)} %collective-permute-done.lower_ref, ...), custom_call_target="tpu_custom_call" | custom-call | tf_op jit(solution)/shard_map/settle_streams/pallas_call | solution.py:228
  36.0 0.0 all-to-all-done
  36.0 7.8 %stream_step.1 = (bf16[128,768]{1,0:T(8,128)(2,1)}, bf16[8,32,768]{2,1,0:T(8,128)(2,1)}, bf16[8,32,768]{2,1,0:T(8,128)(2,1)}, bf16[248,768]{1,0:T(8,128)(2,1)}) custom-call(s32[8]{0:T(128)} %valid_ref.1, bf16[2432,128]{1,0:T(8,128)(2,1)S(1)} %bitcast.9, bf16[8,32,768]{2,1,0:T(8,128)(2,1)S(1)} %get-tuple-element.18.keys_old, ...), custom_call_target="tpu_custom_call" | custom-call | tf_op jit(solution)/shard_map/stream_step/pallas_call | solution.py:423
Async XLA Ops:
  4.0 32.0 %all-to-all-start = ((bf16[16,152,128]{2,1,0:T(8,128)(2,1)}), bf16[16,152,128]{2,1,0:T(8,128)(2,1)S(1)}, u32[]{:S(2)}, u32[]{:S(2)}) async-start(bf16[16,152,128]{2,1,0:T(8,128)(2,1)} %bitcast.4), calls=%async_computation | async-start | bytes 1245184 | tf_op jit(solution)/shard_map/all_to_all | solution.py:469
  11.4 22.4 %collective-permute-start = (bf16[4,96,768]{2,1,0:T(8,128)(2,1)S(1)}, bf16[4,96,768]{2,1,0:T(8,128)(2,1)S(1)}, u32[]{:S(2)}, u32[]{:S(2)}) collective-permute-start(bf16[4,96,768]{2,1,0:T(8,128)(2,1)S(1)} %get-tuple-element.16), channel_id=1, source_target_pairs={{15,0},{0,1},{1,2},{2,3},{3,4},{4,5},{5,6},{6,7},{7,8},{8,9},{9,10... | collective-permute-start | bytes 1769480 | tf_op jit(solution)/shard_map/ppermute | solution.py:451
  11.8 22.0 %collective-permute-start.1 = (bf16[4,96,768]{2,1,0:T(8,128)(2,1)S(1)}, bf16[4,96,768]{2,1,0:T(8,128)(2,1)S(1)}, u32[]{:S(2)}, u32[]{:S(2)}) collective-permute-start(bf16[4,96,768]{2,1,0:T(8,128)(2,1)S(1)} %get-tuple-element.17), channel_id=1, source_target_pairs={{1,0},{2,1},{3,2},{4,3},{5,4},{6,5},{7,6},{8,7},{9,8},{10,9},{11,1... | collective-permute-start | bytes 1769480 | tf_op jit(solution)/shard_map/ppermute | solution.py:451

commit v4 on v3

v4 whole, which is shorter than its diff:
```python
import jax
import jax.numpy as jnp
from jax import lax
from jax.experimental import pallas as pl
from jax.experimental.pallas import tpu as pltpu
from jax.sharding import PartitionSpec as P


HEAD = 96
MIG = 4
EPSILON = 1e-05
LANES = 128
TILE = 8
FOLD = 2
GROUP = 4
SPLIT = 9
CHUNK_EDGES = (0, 3, 6, 8, 9)
AHEAD = 4

BF16 = jnp.bfloat16
F32 = jnp.float32
I32 = jnp.int32


def iota(shape, axis):
    return lax.broadcasted_iota(I32, shape, axis)


def ones_where(condition):
    return jnp.where(condition, 1.0, 0.0).astype(BF16)


def matmul(left, right):
    return jnp.dot(left, right, preferred_element_type=F32)


def matmul_nt(left, right):
    return lax.dot_general(left, right, (((1,), (1,)), ((), ())), preferred_element_type=F32)


def in_vmem(array):
    return pltpu.with_memory_space_constraint(array, pltpu.VMEM)


def in_hbm(array):
    return pltpu.with_memory_space_constraint(array, pltpu.HBM)


def round_up(value, multiple):
    return -(-value // multiple) * multiple


def whole(*spaces):
    return [pl.BlockSpec(memory_space=space) for space in spaces]


def block_sizes(width, capacity):
    slots = round_up(capacity, TILE // FOLD)
    group_rows = FOLD * slots
    groups = width // FOLD // LANES
    return slots, group_rows, groups, groups * group_rows + TILE


def pack_all(
    frames, route_peer, route_pos, destination, key_cache, value_cache, conv_state, peers, capacity
):
    row_count, model = frames.shape
    slots, group_rows, groups, block_rows = block_sizes(model, capacity)
    half = model // FOLD
    streams, left, width = key_cache.shape
    tail = conv_state.shape[0] // streams
    rows = 2 * left + tail + 1

    def body(
        dest_ref, own_ref, peer_ref, pos_ref, key_hbm, value_hbm, conv_hbm, frames_hbm,
        packed_ref, up_ref, down_ref, conv_ref, frames_ref, conv_f32, sems, move_sems,
    ):
        frames_copy = pltpu.make_async_copy(frames_hbm, frames_ref, sems.at[0])
        conv_copy = pltpu.make_async_copy(conv_hbm, conv_ref, sems.at[1])
        frames_copy.start()
        conv_copy.start()
        own = own_ref[0]
        moves = []
        for n, (out_ref, device) in enumerate(
            ((up_ref, (own + 1) % peers), (down_ref, (own + peers - 1) % peers))
        ):
            rank = jnp.int32(0)
            for j in range(streams):
                target = dest_ref[j]
                chosen = target // streams == device
                place = jnp.minimum(rank, MIG - 1)
                copies = [
                    pltpu.make_async_copy(
                        source.at[j],
                        out_ref.at[place, k * left : (k + 1) * left, :],
                        move_sems.at[n, k, j],
                    )
                    for k, source in enumerate((key_hbm, value_hbm))
                ]

                @pl.when(chosen)
                def _():
                    for copy in copies:
                        copy.start()

                moves.append((out_ref, chosen, place, j, target % streams, copies))
                rank = rank + chosen.astype(I32)

        peer = peer_ref[...]
        owner = ones_where(iota((peers, row_count), 0) == peer)
        earlier = ones_where(iota((row_count, row_count), 0) < iota((row_count, row_count), 1))
        running = matmul(owner, earlier)
        slot = jnp.sum(running * owner.astype(F32), axis=0, keepdims=True).astype(I32)
        flat = peer * group_rows + slot
        packed_row = iota((peers * group_rows, row_count), 0)
        pick = jnp.concatenate(
            [ones_where(packed_row == flat + h * slots) for h in range(FOLD)], axis=1
        )
        owner_tile = ones_where(iota((peers * TILE, row_count), 0) // TILE == peer)
        lane = iota((LANES, row_count), 0)
        in_lane = (lane % slots == slot) & (lane < group_rows)
        code = jnp.where(in_lane, (pos_ref[...] + 1).astype(F32), 0.0).astype(BF16)
        codes = matmul_nt(owner_tile, code).astype(BF16)
        frames_copy.wait()
        source = jnp.concatenate(
            [frames_ref[:, h * half : (h + 1) * half] for h in range(FOLD)], axis=0
        )
        packed = matmul(pick, source).astype(BF16)
        for p in range(peers):
            for g in range(groups):
                first = p * block_rows + g * group_rows
                packed_ref[first : first + group_rows, :] = packed[
                    p * group_rows : (p + 1) * group_rows, g * LANES : (g + 1) * LANES
                ]
            packed_ref[(p + 1) * block_rows - TILE : (p + 1) * block_rows, :] = codes[
                p * TILE : (p + 1) * TILE, :
            ]
        conv_copy.wait()
        stream_of = iota((streams, LANES), 0)
        slot_row = jnp.zeros((streams, LANES), I32)
        for j in range(streams):
            slot_row = jnp.where(stream_of == j, dest_ref[j] % streams + 1, slot_row)
        for c in range(width // LANES):
            conv_f32[c, 0 : tail * streams, :] = conv_ref[:, c * LANES : (c + 1) * LANES].astype(F32)
            conv_f32[c, tail * streams : (tail + 1) * streams, :] = slot_row.astype(F32)
        for out_ref in (up_ref, down_ref):
            out_ref[:, 2 * left : rows, :] = jnp.zeros((MIG, 1 + tail, width), BF16)
        for out_ref, chosen, place, j, slot, copies in moves:

            @pl.when(chosen)
            def _():
                for c in range(width // LANES):
                    out_ref[place, 2 * left : rows, c * LANES : (c + 1) * LANES] = conv_f32[
                        c, pl.ds(j, tail + 1, stride=streams), :
                    ].astype(BF16)
                for copy in copies:
                    copy.wait()

    bundle = pltpu.VMEM((MIG, rows, width), BF16)
    return pl.pallas_call(
        body,
        out_shape=(pltpu.VMEM((peers * block_rows, LANES), BF16), bundle, bundle),
        in_specs=whole(*[pltpu.SMEM] * 2, *[pltpu.VMEM] * 2, *[pl.ANY] * 4),
        out_specs=whole(*[pltpu.VMEM] * 3),
        scratch_shapes=[
            pltpu.VMEM(conv_state.shape, BF16),
            pltpu.VMEM(frames.shape, BF16),
            pltpu.VMEM((width // LANES, (tail + 1) * streams, LANES), F32),
            pltpu.SemaphoreType.DMA((2,)),
            pltpu.SemaphoreType.DMA((2, 2, streams)),
        ],
        compiler_params=pltpu.CompilerParams(vmem_limit_bytes=12 << 20),
        name="pack_all",
    )(
        *map(
            in_hbm,
            (
                destination, own_index(), route_peer.reshape(1, -1), route_pos.reshape(1, -1),
                key_cache, value_cache, conv_state, frames,
            ),
        )
    )


def own_index():
    return lax.axis_index("streams").astype(I32).reshape(1)


def valid_tile(valid_ref, streams, lanes):
    stream_of = iota((streams, lanes), 0)
    valid = jnp.zeros((streams, lanes), I32)
    for s in range(streams):
        valid = jnp.where(stream_of == s, valid_ref[s], valid)
    return valid


def settle_streams(
    from_lower, from_upper, destination, valid_count, key_cache, value_cache, conv_state,
    conv_kernel, span,
):
    streams, left, width = key_cache.shape
    tail = conv_state.shape[0] // streams
    taps = conv_kernel.shape[0]
    groups = width // LANES
    cache = (streams, left, width)
    stored = tail + 1

    def body(
        dest_ref, own_ref, valid_ref, lower_ref, upper_ref, key_hbm, value_hbm, conv_hbm, taps_hbm,
        keys_old, values_old, conv_kept, conv_part, taps_f32,
        key_ref, value_ref, conv_ref, taps_ref, conv_f32, conv_old, sems,
    ):
        copies = [
            pltpu.make_async_copy(source, target, sems.at[n])
            for n, (source, target) in enumerate(
                (
                    (conv_hbm, conv_ref), (key_hbm, key_ref), (value_hbm, value_ref),
                    (taps_hbm, taps_ref),
                )
            )
        ]
        for copy in copies:
            copy.start()
        own = own_ref[0]
        codes = [
            (bundle_ref, j, jnp.max(bundle_ref[j, 2 * left + tail :, :].astype(F32)).astype(I32))
            for bundle_ref in (lower_ref, upper_ref)
            for j in range(MIG)
        ]
        valid = valid_tile(valid_ref, streams, streams * stored)
        column = iota((streams, streams * stored), 1)
        first = iota((streams, streams * stored), 0) * stored + valid
        kept_pick = jnp.concatenate(
            [ones_where((column == first + i) & (valid + i < tail)) for i in range(tail)], axis=0
        )
        for bundle_ref, j, code in codes:

            @pl.when(code > 0)
            def _():
                slot = code - 1
                keys_old[slot] = bundle_ref[j, 0:left, :]
                values_old[slot] = bundle_ref[j, left : 2 * left, :]
                for c in range(groups):
                    conv_old[c, pl.ds(pl.multiple_of(slot * stored, TILE), stored), :] = bundle_ref[
                        j, 2 * left : 2 * left + stored, c * LANES : (c + 1) * LANES
                    ].astype(F32)

        for copy in copies:
            copy.wait()
        for c in range(groups):
            lanes = slice(c * LANES, (c + 1) * LANES)
            taps_f32[c] = taps_ref[:, lanes].astype(F32)
            conv_f32[c, 0 : tail * streams, :] = conv_ref[:, lanes].astype(F32)
            conv_f32[c, tail * streams : stored * streams, :] = jnp.zeros((streams, LANES), F32)
        for j in range(streams):
            target = dest_ref[j]

            @pl.when(target // streams == own)
            def _():
                slot = target % streams
                keys_old[slot] = key_ref[j]
                values_old[slot] = value_ref[j]
                for c in range(groups):
                    conv_old[c, pl.ds(pl.multiple_of(slot * stored, TILE), stored), :] = conv_f32[
                        c, pl.ds(j, stored, stride=streams), :
                    ]

        for c in range(groups):
            lanes = slice(c * LANES, (c + 1) * LANES)
            conv_kept[:, lanes] = matmul(kept_pick, conv_old[c].astype(BF16)).astype(BF16)
            inputs = [conv_old[c, pl.ds(j, streams, stride=stored), :] for j in range(tail)]
            totals = [jnp.zeros((streams, LANES), F32)] * span
            for i in range(taps):
                tap = taps_f32[c, pl.ds(i, streams, stride=0), :]
                for t in range(min(span, tail - i)):
                    totals[t] = totals[t] + tap * inputs[t + i]
            for t in range(span):
                conv_part[c, t * streams : (t + 1) * streams, :] = totals[t]

    return pl.pallas_call(
        body,
        out_shape=(
            pltpu.VMEM(cache, BF16),
            pltpu.VMEM(cache, BF16),
            pltpu.VMEM((tail * streams, width), BF16),
            pltpu.VMEM((groups, span * streams, LANES), F32),
            pltpu.VMEM((groups, taps, LANES), F32),
        ),
        in_specs=whole(*[pltpu.SMEM] * 3, *[pltpu.VMEM] * 2, *[pl.ANY] * 4),
        out_specs=whole(*[pltpu.VMEM] * 5),
        scratch_shapes=[
            pltpu.VMEM(cache, BF16),
            pltpu.VMEM(cache, BF16),
            pltpu.VMEM(conv_state.shape, BF16),
            pltpu.VMEM(conv_kernel.shape, BF16),
            pltpu.VMEM((groups, stored * streams, LANES), F32),
            pltpu.VMEM((groups, stored * streams, LANES), F32),
            pltpu.SemaphoreType.DMA((4,)),
        ],
        compiler_params=pltpu.CompilerParams(vmem_limit_bytes=16 << 20),
        name="settle_streams",
    )(
        *map(in_hbm, (destination, own_index(), valid_count)),
        in_vmem(from_lower), in_vmem(from_upper),
        *map(in_hbm, (key_cache, value_cache, conv_state, conv_kernel)),
    )


def stream_step(received, valid_count, settled, qkv_weight, peers, row_count, capacity):
    keys_settled, _, conv_settled, _, taps_settled = settled
    streams, left, width = keys_settled.shape
    tail = conv_settled.shape[0] // streams
    taps = taps_settled.shape[1]
    span = row_count // streams
    model, columns = qkv_weight.shape
    half = model // FOLD
    heads = width // HEAD
    keys = left + span
    lane_groups = width // LANES
    edges = [columns * n // SPLIT for n in CHUNK_EDGES]
    slots, group_rows, groups, block_rows = block_sizes(model, capacity)
    packed_rows = peers * group_rows

    def body(
        valid_ref, recv_ref, keys_old, values_old, conv_kept, conv_part, taps_f32, weight_hbm,
        encoded_hbm, keys_next_hbm, values_next_hbm, conv_next_hbm,
        encoded_ref, keys_next_ref, values_next_ref, conv_next_ref,
        weight_ref, gathered, qkv_ref, attended_ref, attended_f32, encoded_f32,
        weight_sems, out_sems,
    ):
        weight_copies = [
            pltpu.make_async_copy(
                weight_hbm.at[:, first:last], weight_ref.at[:, first:last], weight_sems.at[n]
            )
            for n, (first, last) in enumerate(zip(edges, edges[1:]))
        ]
        out_copies = [
            pltpu.make_async_copy(source, target, out_sems.at[n])
            for n, (source, target) in enumerate(
                (
                    (encoded_ref, encoded_hbm), (keys_next_ref, keys_next_hbm),
                    (values_next_ref, values_next_hbm), (conv_next_ref, conv_next_hbm),
                )
            )
        ]
        for copy in weight_copies[:AHEAD]:
            copy.start()

        for p in range(peers):
            for g in range(groups):
                gathered[p * group_rows : (p + 1) * group_rows, g * LANES : (g + 1) * LANES] = recv_ref[
                    p * block_rows + g * group_rows : p * block_rows + (g + 1) * group_rows, :
                ]
        codes = jnp.concatenate(
            [recv_ref[(p + 1) * block_rows - TILE : (p + 1) * block_rows, :] for p in range(peers)],
            axis=0,
        )
        spread_lane = ones_where(
            iota((LANES, packed_rows), 1) % group_rows == iota((LANES, packed_rows), 0)
        )
        spread = matmul(codes, spread_lane)
        column = iota((peers * TILE, packed_rows), 1)
        own_tile = iota((peers * TILE, packed_rows), 0) == column // group_rows * TILE
        position = jnp.sum(jnp.where(own_tile, spread, 0.0), axis=0, keepdims=True).astype(I32)
        out_row = iota((row_count, packed_rows), 0) + 1
        column_half = iota((row_count, packed_rows), 1) % group_rows // slots
        hit = out_row == position
        place = jnp.concatenate([ones_where(hit & (column_half == h)) for h in range(FOLD)], axis=0)
        halves = matmul(place, gathered[...])
        owned = jnp.concatenate(
            [halves[h * row_count : (h + 1) * row_count, :] for h in range(FOLD)], axis=1
        )
        centered = owned - jnp.mean(owned, axis=-1, keepdims=True)
        spread_of = jnp.mean(centered * centered, axis=-1, keepdims=True)
        normed = (centered * lax.rsqrt(spread_of + EPSILON)).astype(BF16)
        for n, (first, last) in enumerate(zip(edges, edges[1:])):
            weight_copies[n].wait()
            for copy in weight_copies[n + AHEAD : n + AHEAD + 1]:
                copy.start()
            qkv_ref[:, first:last] = matmul(normed, weight_ref[:, first:last]).astype(BF16)

        head_rows = heads * span
        head_mask = ones_where(
            iota((head_rows, width), 1) // HEAD == iota((head_rows, width), 0) // span
        )
        t_of = iota((keys, head_rows), 1) % span
        key_of = iota((keys, head_rows), 0) - left
        causal = key_of <= t_of
        t_row = iota((span, LANES), 0)
        lane = iota((span, LANES), 1)
        all_rows = [slice(s * span, (s + 1) * span) for s in range(streams)]
        all_keys = [
            jnp.concatenate([keys_old[s], qkv_ref[all_rows[s], width : 2 * width]], axis=0)
            for s in range(streams)
        ]
        all_values = [
            jnp.concatenate([values_old[s], qkv_ref[all_rows[s], 2 * width : 3 * width]], axis=0)
            for s in range(streams)
        ]
        all_scores = []
        for first in range(0, streams, 2):
            pair = range(first, first + 2)
            queries = [
                jnp.concatenate([qkv_ref[all_rows[s], 0:width]] * heads, axis=0) * head_mask
                for s in pair
            ]
            scores = matmul_nt(
                jnp.concatenate([all_keys[s] for s in pair], axis=0),
                jnp.concatenate(queries, axis=0),
            )
            all_scores += [
                scores[n * keys : (n + 1) * keys, n * head_rows : (n + 1) * head_rows]
                for n in range(2)
            ]
        all_probabilities = []
        for s in range(streams):
            allowed = (key_of < 0) | (causal & (key_of < valid_ref[s]))
            scores = jnp.where(allowed, all_scores[s] * HEAD ** (-0.5), -1e30)
            weights = jnp.exp(scores - jnp.max(scores, axis=0, keepdims=True))
            all_probabilities.append(
                (weights / jnp.sum(weights, axis=0, keepdims=True)).astype(BF16)
            )
        shift = iota((left, GROUP * keys), 1) - iota((left, GROUP * keys), 0)
        for first in range(0, streams, GROUP):
            group = range(first, first + GROUP)
            pick = jnp.concatenate(
                [ones_where(shift == valid_ref[s] + (s - first) * keys) for s in group], axis=0
            )
            for source, target in ((all_keys, keys_next_ref), (all_values, values_next_ref)):
                target[first * left : (first + GROUP) * left, :] = matmul(
                    pick, jnp.concatenate([source[s] for s in group], axis=0)
                ).astype(BF16)
        out_copies[1].start()
        out_copies[2].start()
        all_mixed = [
            lax.dot_general(
                all_probabilities[s], all_values[s], (((0,), (0,)), ((), ())),
                preferred_element_type=F32,
            )
            for s in range(streams)
        ]
        for s in range(streams):
            for c in range(lane_groups):
                lanes = slice(c * LANES, (c + 1) * LANES)
                first = c * LANES // HEAD
                last = ((c + 1) * LANES - 1) // HEAD
                attended = all_mixed[s][first * span : (first + 1) * span, lanes]
                for h in range(first + 1, last + 1):
                    attended = jnp.where(
                        lane >= h * HEAD - c * LANES,
                        all_mixed[s][h * span : (h + 1) * span, lanes],
                        attended,
                    )
                attended = jnp.where(t_row < valid_ref[s], attended, 0.0).astype(BF16)
                attended_ref[all_rows[s], lanes] = attended
                attended_f32[c, all_rows[s], :] = attended.astype(F32)

        valid = valid_tile(valid_ref, streams, row_count)
        column = iota((streams, row_count), 1)
        frame = valid - tail
        first = iota((streams, row_count), 0) * span + frame
        new_pick = jnp.concatenate(
            [ones_where((column == first + i) & (frame + i >= 0)) for i in range(tail)], axis=0
        )
        conv_next_ref[...] = conv_kept[...] + matmul(new_pick, attended_ref[...]).astype(BF16)
        out_copies[3].start()

        valid = valid_tile(valid_ref, streams, LANES)
        for c in range(lane_groups):
            inputs = [attended_f32[c, pl.ds(t, streams, stride=span), :] for t in range(span)]
            totals = [
                conv_part[c, t * streams : (t + 1) * streams, :] + inputs[t] for t in range(span)
            ]
            for i in range(max(tail - span + 1, 0), taps):
                tap = taps_f32[c, pl.ds(i, streams, stride=0), :]
                for t in range(max(tail - i, 0), min(span, span + tail - i)):
                    totals[t] = totals[t] + tap * inputs[t + i - tail]
            for t in range(span):
                encoded_f32[c, pl.ds(t, streams, stride=span), :] = jnp.where(
                    t < valid, totals[t], 0.0
                )
        for c in range(lane_groups):
            encoded_ref[:, c * LANES : (c + 1) * LANES] = encoded_f32[c].astype(BF16)
        out_copies[0].start()
        for copy in out_copies:
            copy.wait()

    cache = (streams * left, width)
    by_lane_group = pltpu.VMEM((lane_groups, row_count, LANES), F32)
    out_shapes = ((row_count, width), cache, cache, (tail * streams, width))
    return pl.pallas_call(
        body,
        out_shape=[jax.ShapeDtypeStruct(shape, BF16) for shape in out_shapes],
        in_specs=whole(pltpu.SMEM, *[pltpu.VMEM] * 6, pl.ANY),
        out_specs=whole(*[pl.ANY] * 4),
        scratch_shapes=[
            *[pltpu.VMEM(shape, BF16) for shape in out_shapes],
            pltpu.VMEM((model, columns), BF16),
            pltpu.VMEM((packed_rows, half), BF16),
            pltpu.VMEM((row_count, columns), BF16),
            pltpu.VMEM((row_count, width), BF16),
            by_lane_group,
            by_lane_group,
            pltpu.SemaphoreType.DMA((len(edges) - 1,)),
            pltpu.SemaphoreType.DMA((4,)),
        ],
        compiler_params=pltpu.CompilerParams(vmem_limit_bytes=32 << 20),
        name="stream_step",
    )(
        in_hbm(valid_count), in_vmem(received), *map(in_vmem, settled), in_hbm(qkv_weight)
    )


def from_behind(block, axis, distance):
    count = lax.axis_size(axis)
    return lax.ppermute(block, axis, [((i - distance) % count, i) for i in range(count)])


def local(
    frames, route_peer, route_pos, destination, valid_count, key_cache, value_cache, conv_state,
    qkv_weight, conv_kernel,
):
    peers = lax.axis_size("streams")
    row_count = frames.shape[0]
    per_peer = row_count // peers
    capacity = per_peer + per_peer // 2
    streams, left, width = key_cache.shape
    conv_by_time = conv_state.transpose(1, 0, 2).reshape(-1, width)
    packed, up, down = pack_all(
        frames, route_peer, route_pos, destination, key_cache, value_cache, conv_by_time,
        peers, capacity,
    )
    from_lower = from_behind(up, "streams", 1)
    from_upper = from_behind(down, "streams", -1)
    received = lax.all_to_all(packed, "streams", split_axis=0, concat_axis=0, tiled=True)
    settled = settle_streams(
        from_lower, from_upper, destination, valid_count, key_cache, value_cache,
        conv_by_time, conv_kernel, row_count // streams,
    )
    encoded, keys_next, values_next, conv_next = stream_step(
        received, valid_count, settled, qkv_weight, peers, row_count, capacity
    )
    cache = (streams, left, width)
    return (
        encoded, keys_next.reshape(cache), values_next.reshape(cache),
        conv_next.reshape(-1, streams, width).transpose(1, 0, 2),
    )


def solution(mesh):
    rows = P(("groups", "streams"))
    return jax.shard_map(
        local,
        mesh=mesh,
        in_specs=(rows,) * 8 + (P(), P()),
        out_specs=(rows,) * 4,
        check_vma=False,
    )
```

time: 44.1 us -> 45 us (1.020)
  Pallas kernels: 13.4 us -> 14.3 us
    pallas_call x1, Pallas kernels: 2.23 us -> 3.38 us  [settle_streams(): pl.pallas_call(body, out_shape=(pltpu.VMEM(cache, BF16), pltpu.VMEM(cache...]
    pallas_call x1, Pallas kernels: 7.84 us -> 7.24 us  [stream_step(): pl.pallas_call(body, out_shape=[jax.ShapeDtypeStruct(shape, BF16) for sha...]
  transfers between devices with their start and end apart: 3 -> 3, of which waited for: 1 -> 1; matrix products, arithmetic and copies ran while one was open for 0% -> 0% of each run, Pallas kernels for 5% -> 8%
where the time goes in v4:
time: 45 us; the launch traced here: 44.7 us
  waiting for transfers between devices  17.9 us (40%)
  Pallas kernels  14.3 us (32%)
  starting transfers between devices  11.9 us (26%)
  between operations  0.67 us (1%)
    ppermute x2, waiting for transfers between devices, from_behind(): lax.ppermute(block, axis, [((i - distance) % count, i) for i in range(cou...  17.9 us
    all_to_all x1, starting transfers between devices, local(): lax.all_to_all(packed, 'streams', split_axis=0, concat_axis=0, tiled=True)  7.38 us
    pallas_call x1, Pallas kernels, stream_step(): pl.pallas_call(body, out_shape=[jax.ShapeDtypeStruct(shape, BF16) for sha...  7.24 us
    ppermute x2, starting transfers between devices, from_behind(): lax.ppermute(block, axis, [((i - distance) % count, i) for i in range(cou...  4.49 us
    pallas_call x1, Pallas kernels, pack_all(): pl.pallas_call(body, out_shape=(pltpu.VMEM((peers * block_rows, LANES), B...  3.63 us
    pallas_call x1, Pallas kernels, settle_streams(): pl.pallas_call(body, out_shape=(pltpu.VMEM(cache, BF16), pltpu.VMEM(cache...  3.38 us
  transfers between devices with their start and end apart: 3, of which 1 were waited for; matrix products, arithmetic and copies ran while one was open for 0% of the time, Pallas kernels for 8%

profile of v4, /device:TPU:0, one launch (start us, length us, event | category | flops | bytes accessed | tf_op | source)
XLA Modules:
  0.0 44.7 jit_solution(5848943104963218420)
XLA Ops:
  0.6 3.6 %pack_all.1 = (bf16[2432,128]{1,0:T(8,128)(2,1)}, bf16[4,96,768]{2,1,0:T(8,128)(2,1)S(1)}, bf16[4,96,768]{2,1,0:T(8,128)(2,1)S(1)}) custom-call(s32[8]{0:T(128)} %dest_ref.3, s32[1]{0:T(128)} %bitcast.own_ref, s32[1,128]{1,0:T(1,128)} %bitcast.16, s32[1,128]{1,0:T(1,128)} %bitcast.17, bf16[8,32,768]{2,1,0:T(8,128)(2,1)} %key_hbm.3, ...), custom_call_target="tpu_custom_call" | custom-call | tf_op jit(solution)/shard_map/pack_all/pallas_call | solution.py:160
  4.3 7.4 %all-to-all-start = ((bf16[16,152,128]{2,1,0:T(8,128)(2,1)}), bf16[16,152,128]{2,1,0:T(8,128)(2,1)S(1)}, u32[]{:S(2)}, u32[]{:S(2)}) async-start(bf16[16,152,128]{2,1,0:T(8,128)(2,1)} %bitcast.5), calls=%async_computation | async-start | bytes 1245184 | tf_op jit(solution)/shard_map/all_to_all | solution.py:535
  11.7 0.4 collective-permute-start
  12.1 4.1 %collective-permute-start.1 = (bf16[4,96,768]{2,1,0:T(8,128)(2,1)S(1)}, bf16[4,96,768]{2,1,0:T(8,128)(2,1)S(1)}, u32[]{:S(2)}, u32[]{:S(2)}) collective-permute-start(bf16[4,96,768]{2,1,0:T(8,128)(2,1)S(1)} %get-tuple-element.18), channel_id=1, source_target_pairs={{1,0},{2,1},{3,2},{4,3},{5,4},{6,5},{7,6},{8,7},{9,8},{10,9},{11,1... | collective-permute-start | bytes 1769480 | tf_op jit(solution)/shard_map/ppermute | solution.py:516
  16.2 17.9 %collective-permute-done.lower_ref = bf16[4,96,768]{2,1,0:T(8,128)(2,1)S(1)} collective-permute-done((bf16[4,96,768]{2,1,0:T(8,128)(2,1)S(1)}, bf16[4,96,768]{2,1,0:T(8,128)(2,1)S(1)}, u32[]{:S(2)}, u32[]{:S(2)}) %collective-permute-start) | collective-permute-done | bytes 589856 | tf_op jit(solution)/shard_map/ppermute | solution.py:516
  34.0 0.0 collective-permute-done.1.upper_ref
  34.0 3.4 %settle_streams.1 = (bf16[8,32,768]{2,1,0:T(8,128)(2,1)S(1)}, bf16[8,32,768]{2,1,0:T(8,128)(2,1)S(1)}, bf16[248,768]{1,0:T(8,128)(2,1)S(1)}, f32[6,128,128]{2,1,0:T(8,128)S(1)}, f32[6,32,128]{2,1,0:T(8,128)S(1)}) custom-call(s32[8]{0:T(128)} %dest_ref.3, s32[1]{0:T(128)} %bitcast.own_ref, s32[8]{0:T(128)} %valid_ref.3, ...), custom_call_target="tpu_custom_call" | custom-call | tf_op jit(solution)/shard_map/settle_streams/pallas_call | solution.py:280
  37.4 0.0 all-to-all-done
  37.4 7.2 %stream_step.1 = (bf16[128,768]{1,0:T(8,128)(2,1)}, bf16[256,768]{1,0:T(8,128)(2,1)}, bf16[256,768]{1,0:T(8,128)(2,1)}, bf16[248,768]{1,0:T(8,128)(2,1)}) custom-call(s32[8]{0:T(128)} %valid_ref.3, bf16[2432,128]{1,0:T(8,128)(2,1)S(1)} %bitcast.13, bf16[8,32,768]{2,1,0:T(8,128)(2,1)S(1)} %get-tuple-element.19.keys_old, ...), custom_call_target="tpu_custom_call" | custom-call | tf_op jit(solution)/shard_map/stream_step/pallas_call | solution.py:491
Async XLA Ops:
  4.3 33.1 %all-to-all-start = ((bf16[16,152,128]{2,1,0:T(8,128)(2,1)}), bf16[16,152,128]{2,1,0:T(8,128)(2,1)S(1)}, u32[]{:S(2)}, u32[]{:S(2)}) async-start(bf16[16,152,128]{2,1,0:T(8,128)(2,1)} %bitcast.5), calls=%async_computation | async-start | bytes 1245184 | tf_op jit(solution)/shard_map/all_to_all | solution.py:535
  11.7 22.4 %collective-permute-start = (bf16[4,96,768]{2,1,0:T(8,128)(2,1)S(1)}, bf16[4,96,768]{2,1,0:T(8,128)(2,1)S(1)}, u32[]{:S(2)}, u32[]{:S(2)}) collective-permute-start(bf16[4,96,768]{2,1,0:T(8,128)(2,1)S(1)} %get-tuple-element.17), channel_id=1, source_target_pairs={{15,0},{0,1},{1,2},{2,3},{3,4},{4,5},{5,6},{6,7},{7,8},{8,9},{9,10... | collective-permute-start | bytes 1769480 | tf_op jit(solution)/shard_map/ppermute | solution.py:516
  12.1 22.0 %collective-permute-start.1 = (bf16[4,96,768]{2,1,0:T(8,128)(2,1)S(1)}, bf16[4,96,768]{2,1,0:T(8,128)(2,1)S(1)}, u32[]{:S(2)}, u32[]{:S(2)}) collective-permute-start(bf16[4,96,768]{2,1,0:T(8,128)(2,1)S(1)} %get-tuple-element.18), channel_id=1, source_target_pairs={{1,0},{2,1},{3,2},{4,3},{5,4},{6,5},{7,6},{8,7},{9,8},{10,9},{11,1... | collective-permute-start | bytes 1769480 | tf_op jit(solution)/shard_map/ppermute | solution.py:516

commit v5 on v4

--- a/solution.py
+++ b/solution.py
@@ -14,8 +14,9 @@
 FOLD = 2
 GROUP = 4
 SPLIT = 9
-CHUNK_EDGES = (0, 3, 6, 8, 9)
-AHEAD = 4
+CHUNK_EDGES = (0, 3, 6, 9)
+VALUES_FROM = 2
+PIECE = 6
 
 BF16 = jnp.bfloat16
 F32 = jnp.float32
@@ -44,6 +45,16 @@
 
 def in_hbm(array):
     return pltpu.with_memory_space_constraint(array, pltpu.HBM)
+
+
+def start_copies(pairs, sems):
+    copies = [
+        pltpu.make_async_copy(source, target, sems.at[n])
+        for n, (source, target) in enumerate(pairs)
+    ]
+    for copy in copies:
+        copy.start()
+    return copies
 
 
 def round_up(value, multiple):
@@ -72,13 +83,20 @@
     rows = 2 * left + tail + 1
 
     def body(
-        dest_ref, own_ref, peer_ref, pos_ref, key_hbm, value_hbm, conv_hbm, frames_hbm,
-        packed_ref, up_ref, down_ref, conv_ref, frames_ref, conv_f32, sems, move_sems,
+        dest_hbm, own_hbm, peer_hbm, pos_hbm, key_hbm, value_hbm, conv_hbm, frames_hbm,
+        packed_hbm, up_ref, down_ref, packed_ref, conv_ref, frames_ref, conv_f32, dest_ref, own_ref,
+        peer_ref, pos_ref, sems, small_sems, move_sems,
     ):
         frames_copy = pltpu.make_async_copy(frames_hbm, frames_ref, sems.at[0])
         conv_copy = pltpu.make_async_copy(conv_hbm, conv_ref, sems.at[1])
+        small_copies = start_copies(
+            ((peer_hbm, peer_ref), (pos_hbm, pos_ref), (dest_hbm, dest_ref), (own_hbm, own_ref)),
+            small_sems,
+        )
         frames_copy.start()
         conv_copy.start()
+        for copy in small_copies:
+            copy.wait()
         own = own_ref[0]
         moves = []
         for n, (out_ref, device) in enumerate(
@@ -135,6 +153,8 @@
             packed_ref[(p + 1) * block_rows - TILE : (p + 1) * block_rows, :] = codes[
                 p * TILE : (p + 1) * TILE, :
             ]
+        packed_copy = pltpu.make_async_copy(packed_ref, packed_hbm, sems.at[2])
+        packed_copy.start()
         conv_copy.wait()
         stream_of = iota((streams, LANES), 0)
         slot_row = jnp.zeros((streams, LANES), I32)
@@ -156,17 +176,26 @@
                 for copy in copies:
                     copy.wait()
 
+        packed_copy.wait()
+
+    packed_shape = (peers * block_rows, LANES)
     bundle = pltpu.VMEM((MIG, rows, width), BF16)
     return pl.pallas_call(
         body,
-        out_shape=(pltpu.VMEM((peers * block_rows, LANES), BF16), bundle, bundle),
-        in_specs=whole(*[pltpu.SMEM] * 2, *[pltpu.VMEM] * 2, *[pl.ANY] * 4),
-        out_specs=whole(*[pltpu.VMEM] * 3),
+        out_shape=(pltpu.HBM(packed_shape, BF16), bundle, bundle),
+        in_specs=whole(*[pl.ANY] * 8),
+        out_specs=whole(pl.ANY, pltpu.VMEM, pltpu.VMEM),
         scratch_shapes=[
+            pltpu.VMEM(packed_shape, BF16),
             pltpu.VMEM(conv_state.shape, BF16),
             pltpu.VMEM(frames.shape, BF16),
             pltpu.VMEM((width // LANES, (tail + 1) * streams, LANES), F32),
-            pltpu.SemaphoreType.DMA((2,)),
+            pltpu.SMEM((streams,), I32),
+            pltpu.SMEM((1,), I32),
+            pltpu.VMEM((1, row_count), I32),
+            pltpu.VMEM((1, row_count), I32),
+            pltpu.SemaphoreType.DMA((3,)),
+            pltpu.SemaphoreType.DMA((4,)),
             pltpu.SemaphoreType.DMA((2, 2, streams)),
         ],
         compiler_params=pltpu.CompilerParams(vmem_limit_bytes=12 << 20),
@@ -206,27 +235,29 @@
     stored = tail + 1
 
     def body(
-        dest_ref, own_ref, valid_ref, lower_ref, upper_ref, key_hbm, value_hbm, conv_hbm, taps_hbm,
+        dest_hbm, own_hbm, valid_hbm, lower_ref, upper_ref, key_hbm, value_hbm, conv_hbm, taps_hbm,
         keys_old, values_old, conv_kept, conv_part, taps_f32,
-        key_ref, value_ref, conv_ref, taps_ref, conv_f32, conv_old, sems,
+        key_ref, value_ref, conv_ref, taps_ref, conv_f32, conv_old, dest_ref, own_ref, valid_ref,
+        sems, small_sems,
     ):
-        copies = [
-            pltpu.make_async_copy(source, target, sems.at[n])
-            for n, (source, target) in enumerate(
-                (
-                    (conv_hbm, conv_ref), (key_hbm, key_ref), (value_hbm, value_ref),
-                    (taps_hbm, taps_ref),
-                )
-            )
-        ]
-        for copy in copies:
-            copy.start()
-        own = own_ref[0]
+        small_copies = start_copies(
+            ((dest_hbm, dest_ref), (own_hbm, own_ref), (valid_hbm, valid_ref)), small_sems
+        )
+        copies = start_copies(
+            (
+                (conv_hbm, conv_ref), (key_hbm, key_ref), (value_hbm, value_ref),
+                (taps_hbm, taps_ref),
+            ),
+            sems,
+        )
         codes = [
             (bundle_ref, j, jnp.max(bundle_ref[j, 2 * left + tail :, :].astype(F32)).astype(I32))
             for bundle_ref in (lower_ref, upper_ref)
             for j in range(MIG)
         ]
+        for copy in small_copies:
+            copy.wait()
+        own = own_ref[0]
         valid = valid_tile(valid_ref, streams, streams * stored)
         column = iota((streams, streams * stored), 1)
         first = iota((streams, streams * stored), 0) * stored + valid
@@ -286,7 +317,7 @@
             pltpu.VMEM((groups, span * streams, LANES), F32),
             pltpu.VMEM((groups, taps, LANES), F32),
         ),
-        in_specs=whole(*[pltpu.SMEM] * 3, *[pltpu.VMEM] * 2, *[pl.ANY] * 4),
+        in_specs=whole(*[pl.ANY] * 3, *[pltpu.VMEM] * 2, *[pl.ANY] * 4),
         out_specs=whole(*[pltpu.VMEM] * 5),
         scratch_shapes=[
             pltpu.VMEM(cache, BF16),
@@ -295,7 +326,11 @@
             pltpu.VMEM(conv_kernel.shape, BF16),
             pltpu.VMEM((groups, stored * streams, LANES), F32),
             pltpu.VMEM((groups, stored * streams, LANES), F32),
+            pltpu.SMEM((streams,), I32),
+            pltpu.SMEM((1,), I32),
+            pltpu.SMEM((streams,), I32),
             pltpu.SemaphoreType.DMA((4,)),
+            pltpu.SemaphoreType.DMA((3,)),
         ],
         compiler_params=pltpu.CompilerParams(vmem_limit_bytes=16 << 20),
         name="settle_streams",
@@ -322,11 +357,11 @@
     packed_rows = peers * group_rows
 
     def body(
-        valid_ref, recv_ref, keys_old, values_old, conv_kept, conv_part, taps_f32, weight_hbm,
+        valid_hbm, recv_ref, keys_old, values_old, conv_kept, conv_part, taps_f32, weight_hbm,
         encoded_hbm, keys_next_hbm, values_next_hbm, conv_next_hbm,
         encoded_ref, keys_next_ref, values_next_ref, conv_next_ref,
-        weight_ref, gathered, qkv_ref, attended_ref, attended_f32, encoded_f32,
-        weight_sems, out_sems,
+        weight_ref, gathered, qkv_ref, attended_ref, attended_f32, encoded_f32, valid_ref,
+        weight_sems, out_sems, valid_sem,
     ):
         weight_copies = [
             pltpu.make_async_copy(
@@ -334,17 +369,10 @@
             )
             for n, (first, last) in enumerate(zip(edges, edges[1:]))
         ]
-        out_copies = [
-            pltpu.make_async_copy(source, target, out_sems.at[n])
-            for n, (source, target) in enumerate(
-                (
-                    (encoded_ref, encoded_hbm), (keys_next_ref, keys_next_hbm),
-                    (values_next_ref, values_next_hbm), (conv_next_ref, conv_next_hbm),
-                )
-            )
-        ]
-        for copy in weight_copies[:AHEAD]:
+        for copy in weight_copies:
             copy.start()
+        valid_copy = pltpu.make_async_copy(valid_hbm, valid_ref, valid_sem)
+        valid_copy.start()
 
         for p in range(peers):
             for g in range(groups):
@@ -373,11 +401,15 @@
         centered = owned - jnp.mean(owned, axis=-1, keepdims=True)
         spread_of = jnp.mean(centered * centered, axis=-1, keepdims=True)
         normed = (centered * lax.rsqrt(spread_of + EPSILON)).astype(BF16)
-        for n, (first, last) in enumerate(zip(edges, edges[1:])):
+
+        def project(n):
             weight_copies[n].wait()
-            for copy in weight_copies[n + AHEAD : n + AHEAD + 1]:
-                copy.start()
-            qkv_ref[:, first:last] = matmul(normed, weight_ref[:, first:last]).astype(BF16)
+            columns_of = slice(edges[n], edges[n + 1])
+            qkv_ref[:, columns_of] = matmul(normed, weight_ref[:, columns_of]).astype(BF16)
+
+        for n in range(VALUES_FROM):
+            project(n)
+        valid_copy.wait()
 
         head_rows = heads * span
         head_mask = ones_where(
@@ -391,10 +423,6 @@
         all_rows = [slice(s * span, (s + 1) * span) for s in range(streams)]
         all_keys = [
             jnp.concatenate([keys_old[s], qkv_ref[all_rows[s], width : 2 * width]], axis=0)
-            for s in range(streams)
-        ]
-        all_values = [
-            jnp.concatenate([values_old[s], qkv_ref[all_rows[s], 2 * width : 3 * width]], axis=0)
             for s in range(streams)
         ]
         all_scores = []
@@ -421,40 +449,24 @@
                 (weights / jnp.sum(weights, axis=0, keepdims=True)).astype(BF16)
             )
         shift = iota((left, GROUP * keys), 1) - iota((left, GROUP * keys), 0)
-        for first in range(0, streams, GROUP):
-            group = range(first, first + GROUP)
-            pick = jnp.concatenate(
-                [ones_where(shift == valid_ref[s] + (s - first) * keys) for s in group], axis=0
+        groups_of = [range(first, first + GROUP) for first in range(0, streams, GROUP)]
+        picks = [
+            jnp.concatenate(
+                [ones_where(shift == valid_ref[s] + n * keys) for n, s in enumerate(group)], axis=0
             )
-            for source, target in ((all_keys, keys_next_ref), (all_values, values_next_ref)):
-                target[first * left : (first + GROUP) * left, :] = matmul(
+            for group in groups_of
+        ]
+
+        def shifted(source, target):
+            for group, pick in zip(groups_of, picks):
+                target[group[0] * left : (group[-1] + 1) * left, :] = matmul(
                     pick, jnp.concatenate([source[s] for s in group], axis=0)
                 ).astype(BF16)
-        out_copies[1].start()
-        out_copies[2].start()
-        all_mixed = [
-            lax.dot_general(
-                all_probabilities[s], all_values[s], (((0,), (0,)), ((), ())),
-                preferred_element_type=F32,
-            )
-            for s in range(streams)
-        ]
-        for s in range(streams):
-            for c in range(lane_groups):
-                lanes = slice(c * LANES, (c + 1) * LANES)
-                first = c * LANES // HEAD
-                last = ((c + 1) * LANES - 1) // HEAD
-                attended = all_mixed[s][first * span : (first + 1) * span, lanes]
-                for h in range(first + 1, last + 1):
-                    attended = jnp.where(
-                        lane >= h * HEAD - c * LANES,
-                        all_mixed[s][h * span : (h + 1) * span, lanes],
-                        attended,
-                    )
-                attended = jnp.where(t_row < valid_ref[s], attended, 0.0).astype(BF16)
-                attended_ref[all_rows[s], lanes] = attended
-                attended_f32[c, all_rows[s], :] = attended.astype(F32)
-
+
+        shifted(all_keys, keys_next_ref)
+        keys_copy = pltpu.make_async_copy(keys_next_ref, keys_next_hbm, out_sems.at[0])
+        keys_copy.start()
+        out_copies = [keys_copy]
         valid = valid_tile(valid_ref, streams, row_count)
         column = iota((streams, row_count), 1)
         frame = valid - tail
@@ -462,26 +474,77 @@
         new_pick = jnp.concatenate(
             [ones_where((column == first + i) & (frame + i >= 0)) for i in range(tail)], axis=0
         )
-        conv_next_ref[...] = conv_kept[...] + matmul(new_pick, attended_ref[...]).astype(BF16)
-        out_copies[3].start()
-
         valid = valid_tile(valid_ref, streams, LANES)
-        for c in range(lane_groups):
-            inputs = [attended_f32[c, pl.ds(t, streams, stride=span), :] for t in range(span)]
-            totals = [
-                conv_part[c, t * streams : (t + 1) * streams, :] + inputs[t] for t in range(span)
+
+        for piece in range(lane_groups // PIECE):
+            project(VALUES_FROM + piece)
+            lanes = slice(piece * PIECE * LANES, (piece + 1) * PIECE * LANES)
+            all_values = [
+                jnp.concatenate(
+                    [
+                        values_old[s, :, lanes],
+                        qkv_ref[all_rows[s], 2 * width + lanes.start : 2 * width + lanes.stop],
+                    ],
+                    axis=0,
+                )
+                for s in range(streams)
             ]
-            for i in range(max(tail - span + 1, 0), taps):
-                tap = taps_f32[c, pl.ds(i, streams, stride=0), :]
-                for t in range(max(tail - i, 0), min(span, span + tail - i)):
-                    totals[t] = totals[t] + tap * inputs[t + i - tail]
-            for t in range(span):
-                encoded_f32[c, pl.ds(t, streams, stride=span), :] = jnp.where(
-                    t < valid, totals[t], 0.0
+            all_mixed = [
+                lax.dot_general(
+                    all_probabilities[s], all_values[s], (((0,), (0,)), ((), ())),
+                    preferred_element_type=F32,
                 )
-        for c in range(lane_groups):
-            encoded_ref[:, c * LANES : (c + 1) * LANES] = encoded_f32[c].astype(BF16)
-        out_copies[0].start()
+                for s in range(streams)
+            ]
+            for group, pick in zip(groups_of, picks):
+                values_next_ref[group[0] * left : (group[-1] + 1) * left, lanes] = matmul(
+                    pick, jnp.concatenate([all_values[s] for s in group], axis=0)
+                ).astype(BF16)
+            for s in range(streams):
+                for n in range(PIECE):
+                    c = piece * PIECE + n
+                    here = slice(n * LANES, (n + 1) * LANES)
+                    first = c * LANES // HEAD
+                    last = ((c + 1) * LANES - 1) // HEAD
+                    attended = all_mixed[s][first * span : (first + 1) * span, here]
+                    for h in range(first + 1, last + 1):
+                        attended = jnp.where(
+                            lane >= h * HEAD - c * LANES,
+                            all_mixed[s][h * span : (h + 1) * span, here],
+                            attended,
+                        )
+                    attended = jnp.where(t_row < valid_ref[s], attended, 0.0).astype(BF16)
+                    attended_ref[all_rows[s], c * LANES : (c + 1) * LANES] = attended
+                    attended_f32[c, all_rows[s], :] = attended.astype(F32)
+            conv_next_ref[:, lanes] = conv_kept[:, lanes] + matmul(
+                new_pick, attended_ref[:, lanes]
+            ).astype(BF16)
+            for c in range(piece * PIECE, (piece + 1) * PIECE):
+                inputs = [attended_f32[c, pl.ds(t, streams, stride=span), :] for t in range(span)]
+                totals = [
+                    conv_part[c, t * streams : (t + 1) * streams, :] + inputs[t]
+                    for t in range(span)
+                ]
+                for i in range(max(tail - span + 1, 0), taps):
+                    tap = taps_f32[c, pl.ds(i, streams, stride=0), :]
+                    for t in range(max(tail - i, 0), min(span, span + tail - i)):
+                        totals[t] = totals[t] + tap * inputs[t + i - tail]
+                for t in range(span):
+                    encoded_f32[c, pl.ds(t, streams, stride=span), :] = jnp.where(
+                        t < valid, totals[t], 0.0
+                    )
+                encoded_ref[:, c * LANES : (c + 1) * LANES] = encoded_f32[c].astype(BF16)
+            for n, (source, target) in enumerate(
+                (
+                    (values_next_ref, values_next_hbm), (conv_next_ref, conv_next_hbm),
+                    (encoded_ref, encoded_hbm),
+                )
+            ):
+                copy = pltpu.make_async_copy(
+                    source.at[:, lanes], target.at[:, lanes], out_sems.at[1 + 3 * piece + n]
+                )
+                copy.start()
+                out_copies.append(copy)
         for copy in out_copies:
             copy.wait()
 
@@ -491,7 +554,7 @@
     return pl.pallas_call(
         body,
         out_shape=[jax.ShapeDtypeStruct(shape, BF16) for shape in out_shapes],
-        in_specs=whole(pltpu.SMEM, *[pltpu.VMEM] * 6, pl.ANY),
+        in_specs=whole(pl.ANY, *[pltpu.VMEM] * 6, pl.ANY),
         out_specs=whole(*[pl.ANY] * 4),
         scratch_shapes=[
             *[pltpu.VMEM(shape, BF16) for shape in out_shapes],
@@ -501,8 +564,10 @@
             pltpu.VMEM((row_count, width), BF16),
             by_lane_group,
             by_lane_group,
+            pltpu.SMEM((streams,), I32),
             pltpu.SemaphoreType.DMA((len(edges) - 1,)),
-            pltpu.SemaphoreType.DMA((4,)),
+            pltpu.SemaphoreType.DMA((1 + 3 * (lane_groups // PIECE),)),
+            pltpu.SemaphoreType.DMA,
         ],
         compiler_params=pltpu.CompilerParams(vmem_limit_bytes=32 << 20),
         name="stream_step",

time: 45 us -> 42.8 us (0.951)
  Pallas kernels: 14.3 us -> 12.1 us
    pallas_call x1, Pallas kernels: 3.63 us -> 2.63 us  [pack_all(): pl.pallas_call(body, out_shape=(pltpu.HBM(packed_shape, BF16), bundle, bu...]
    pallas_call x1, Pallas kernels: 3.38 us -> 2.73 us  [settle_streams(): pl.pallas_call(body, out_shape=(pltpu.VMEM(cache, BF16), pltpu.VMEM(cache...]
    pallas_call x1, Pallas kernels: 7.24 us -> 6.7 us  [stream_step(): pl.pallas_call(body, out_shape=[jax.ShapeDtypeStruct(shape, BF16) for sha...]
  transfers between devices with their start and end apart: 3 -> 3, of which waited for: 1 -> 1; matrix products, arithmetic and copies ran while one was open for 0% -> 0% of each run, Pallas kernels for 8% -> 6%
where the time goes in v5:
time: 42.8 us; the launch traced here: 42.5 us
  waiting for transfers between devices  17.9 us (42%)
  Pallas kernels  12.1 us (28%)
  starting transfers between devices  11.9 us (28%)
  between operations  0.67 us (2%)
    ppermute x2, waiting for transfers between devices, from_behind(): lax.ppermute(block, axis, [((i - distance) % count, i) for i in range(cou...  17.9 us
    all_to_all x1, starting transfers between devices, local(): lax.all_to_all(packed, 'streams', split_axis=0, concat_axis=0, tiled=True)  7.43 us
    pallas_call x1, Pallas kernels, stream_step(): pl.pallas_call(body, out_shape=[jax.ShapeDtypeStruct(shape, BF16) for sha...  6.7 us
    ppermute x2, starting transfers between devices, from_behind(): lax.ppermute(block, axis, [((i - distance) % count, i) for i in range(cou...  4.49 us
    pallas_call x1, Pallas kernels, settle_streams(): pl.pallas_call(body, out_shape=(pltpu.VMEM(cache, BF16), pltpu.VMEM(cache...  2.73 us
    pallas_call x1, Pallas kernels, pack_all(): pl.pallas_call(body, out_shape=(pltpu.HBM(packed_shape, BF16), bundle, bu...  2.63 us
  transfers between devices with their start and end apart: 3, of which 1 were waited for; matrix products, arithmetic and copies ran while one was open for 0% of the time, Pallas kernels for 6%

profile of v5, /device:TPU:0, one launch (start us, length us, event | category | flops | bytes accessed | tf_op | source)
XLA Modules:
  0.0 42.5 jit_solution(6062325532939577755)
XLA Ops:
  0.6 2.6 %pack_all.1 = (bf16[2432,128]{1,0:T(8,128)(2,1)}, bf16[4,96,768]{2,1,0:T(8,128)(2,1)S(1)}, bf16[4,96,768]{2,1,0:T(8,128)(2,1)S(1)}) custom-call(s32[8]{0:T(128)} %dest_hbm.3, s32[1]{0:T(128)} %bitcast.own_hbm, s32[1,128]{1,0:T(1,128)} %bitcast.17, s32[1,128]{1,0:T(1,128)} %bitcast.18, bf16[8,32,768]{2,1,0:T(8,128)(2,1)} %key_hbm.3, ...), custom_call_target="tpu_custom_call" | custom-call | tf_op jit(solution)/shard_map/pack_all/pallas_call | solution.py:183
  3.3 7.4 %all-to-all-start = ((bf16[16,152,128]{2,1,0:T(8,128)(2,1)}), bf16[16,152,128]{2,1,0:T(8,128)(2,1)S(1)}, u32[]{:S(2)}, u32[]{:S(2)}) async-start(bf16[16,152,128]{2,1,0:T(8,128)(2,1)} %bitcast.16), calls=%async_computation | async-start | bytes 1245184 | tf_op jit(solution)/shard_map/all_to_all | solution.py:600
  10.7 0.4 collective-permute-start
  11.1 4.1 %collective-permute-start.1 = (bf16[4,96,768]{2,1,0:T(8,128)(2,1)S(1)}, bf16[4,96,768]{2,1,0:T(8,128)(2,1)S(1)}, u32[]{:S(2)}, u32[]{:S(2)}) collective-permute-start(bf16[4,96,768]{2,1,0:T(8,128)(2,1)S(1)} %get-tuple-element.18), channel_id=1, source_target_pairs={{1,0},{2,1},{3,2},{4,3},{5,4},{6,5},{7,6},{8,7},{9,8},{10,9},{11,1... | collective-permute-start | bytes 1769480 | tf_op jit(solution)/shard_map/ppermute | solution.py:581
  15.2 17.9 %collective-permute-done.lower_ref = bf16[4,96,768]{2,1,0:T(8,128)(2,1)S(1)} collective-permute-done((bf16[4,96,768]{2,1,0:T(8,128)(2,1)S(1)}, bf16[4,96,768]{2,1,0:T(8,128)(2,1)S(1)}, u32[]{:S(2)}, u32[]{:S(2)}) %collective-permute-start) | collective-permute-done | bytes 589856 | tf_op jit(solution)/shard_map/ppermute | solution.py:581
  33.1 0.0 collective-permute-done.1.upper_ref
  33.1 2.7 %settle_streams.1 = (bf16[8,32,768]{2,1,0:T(8,128)(2,1)S(1)}, bf16[8,32,768]{2,1,0:T(8,128)(2,1)S(1)}, bf16[248,768]{1,0:T(8,128)(2,1)S(1)}, f32[6,128,128]{2,1,0:T(8,128)S(1)}, f32[6,32,128]{2,1,0:T(8,128)S(1)}) custom-call(s32[8]{0:T(128)} %dest_hbm.3, s32[1]{0:T(128)} %bitcast.own_hbm, s32[8]{0:T(128)} %valid_hbm.3, ...), custom_call_target="tpu_custom_call" | custom-call | tf_op jit(solution)/shard_map/settle_streams/pallas_call | solution.py:311
  35.8 0.0 all-to-all-done
  35.8 6.7 %stream_step.1 = (bf16[128,768]{1,0:T(8,128)(2,1)}, bf16[256,768]{1,0:T(8,128)(2,1)}, bf16[256,768]{1,0:T(8,128)(2,1)}, bf16[248,768]{1,0:T(8,128)(2,1)}) custom-call(s32[8]{0:T(128)} %valid_hbm.3, bf16[2432,128]{1,0:T(8,128)(2,1)S(1)} %bitcast.13, bf16[8,32,768]{2,1,0:T(8,128)(2,1)S(1)} %get-tuple-element.19.keys_old, ...), custom_call_target="tpu_custom_call" | custom-call | tf_op jit(solution)/shard_map/stream_step/pallas_call | solution.py:554
Async XLA Ops:
  3.3 32.5 %all-to-all-start = ((bf16[16,152,128]{2,1,0:T(8,128)(2,1)}), bf16[16,152,128]{2,1,0:T(8,128)(2,1)S(1)}, u32[]{:S(2)}, u32[]{:S(2)}) async-start(bf16[16,152,128]{2,1,0:T(8,128)(2,1)} %bitcast.16), calls=%async_computation | async-start | bytes 1245184 | tf_op jit(solution)/shard_map/all_to_all | solution.py:600
  10.7 22.4 %collective-permute-start = (bf16[4,96,768]{2,1,0:T(8,128)(2,1)S(1)}, bf16[4,96,768]{2,1,0:T(8,128)(2,1)S(1)}, u32[]{:S(2)}, u32[]{:S(2)}) collective-permute-start(bf16[4,96,768]{2,1,0:T(8,128)(2,1)S(1)} %get-tuple-element.17), channel_id=1, source_target_pairs={{15,0},{0,1},{1,2},{2,3},{3,4},{4,5},{5,6},{6,7},{7,8},{8,9},{9,10... | collective-permute-start | bytes 1769480 | tf_op jit(solution)/shard_map/ppermute | solution.py:581
  11.1 22.0 %collective-permute-start.1 = (bf16[4,96,768]{2,1,0:T(8,128)(2,1)S(1)}, bf16[4,96,768]{2,1,0:T(8,128)(2,1)S(1)}, u32[]{:S(2)}, u32[]{:S(2)}) collective-permute-start(bf16[4,96,768]{2,1,0:T(8,128)(2,1)S(1)} %get-tuple-element.18), channel_id=1, source_target_pairs={{1,0},{2,1},{3,2},{4,3},{5,4},{6,5},{7,6},{8,7},{9,8},{10,9},{11,1... | collective-permute-start | bytes 1769480 | tf_op jit(solution)/shard_map/ppermute | solution.py:581

commit v6 on v5

--- a/solution.py
+++ b/solution.py
@@ -225,9 +225,10 @@
 
 def settle_streams(
     from_lower, from_upper, destination, valid_count, key_cache, value_cache, conv_state,
-    conv_kernel, span,
+    conv_kernel, qkv_weight, span,
 ):
     streams, left, width = key_cache.shape
+    block = from_lower.shape[1]
     tail = conv_state.shape[0] // streams
     taps = conv_kernel.shape[0]
     groups = width // LANES
@@ -236,9 +237,9 @@
 
     def body(
         dest_hbm, own_hbm, valid_hbm, lower_ref, upper_ref, key_hbm, value_hbm, conv_hbm, taps_hbm,
-        keys_old, values_old, conv_kept, conv_part, taps_f32,
+        weight_hbm, keys_old, values_old, conv_kept, conv_part, taps_f32, first_weight, second_weight,
         key_ref, value_ref, conv_ref, taps_ref, conv_f32, conv_old, dest_ref, own_ref, valid_ref,
-        sems, small_sems,
+        sems, small_sems, weight_sems,
     ):
         small_copies = start_copies(
             ((dest_hbm, dest_ref), (own_hbm, own_ref), (valid_hbm, valid_ref)), small_sems
@@ -276,6 +277,14 @@
                         j, 2 * left : 2 * left + stored, c * LANES : (c + 1) * LANES
                     ].astype(F32)
 
+        weight_copies = start_copies(
+            [
+                (weight_hbm.at[(n * MIG + j) * block : (n * MIG + j + 1) * block, 0:width], target.at[j])
+                for n, target in enumerate((first_weight, second_weight))
+                for j in range(MIG)
+            ],
+            weight_sems,
+        )
         for copy in copies:
             copy.wait()
         for c in range(groups):
@@ -307,6 +316,8 @@
                     totals[t] = totals[t] + tap * inputs[t + i]
             for t in range(span):
                 conv_part[c, t * streams : (t + 1) * streams, :] = totals[t]
+        for copy in weight_copies:
+            copy.wait()
 
     return pl.pallas_call(
         body,
@@ -316,9 +327,12 @@
             pltpu.VMEM((tail * streams, width), BF16),
             pltpu.VMEM((groups, span * streams, LANES), F32),
             pltpu.VMEM((groups, taps, LANES), F32),
+            pltpu.VMEM(from_lower.shape, BF16),
+            pltpu.VMEM(from_lower.shape, BF16),
         ),
-        in_specs=whole(*[pl.ANY] * 3, *[pltpu.VMEM] * 2, *[pl.ANY] * 4),
-        out_specs=whole(*[pltpu.VMEM] * 5),
+        in_specs=whole(*[pl.ANY] * 3, *[pltpu.VMEM] * 2, *[pl.ANY] * 5),
+        out_specs=whole(*[pltpu.VMEM] * 7),
+        input_output_aliases={3: 5, 4: 6},
         scratch_shapes=[
             pltpu.VMEM(cache, BF16),
             pltpu.VMEM(cache, BF16),
@@ -331,18 +345,20 @@
             pltpu.SMEM((streams,), I32),
             pltpu.SemaphoreType.DMA((4,)),
             pltpu.SemaphoreType.DMA((3,)),
+            pltpu.SemaphoreType.DMA((2 * MIG,)),
         ],
         compiler_params=pltpu.CompilerParams(vmem_limit_bytes=16 << 20),
         name="settle_streams",
     )(
         *map(in_hbm, (destination, own_index(), valid_count)),
         in_vmem(from_lower), in_vmem(from_upper),
-        *map(in_hbm, (key_cache, value_cache, conv_state, conv_kernel)),
+        *map(in_hbm, (key_cache, value_cache, conv_state, conv_kernel, qkv_weight)),
     )
 
 
 def stream_step(received, valid_count, settled, qkv_weight, peers, row_count, capacity):
-    keys_settled, _, conv_settled, _, taps_settled = settled
+    keys_settled, _, conv_settled, _, taps_settled, near_weight, _ = settled
+    near = near_weight.shape[0] * near_weight.shape[1]
     streams, left, width = keys_settled.shape
     tail = conv_settled.shape[0] // streams
     taps = taps_settled.shape[1]
@@ -357,17 +373,19 @@
     packed_rows = peers * group_rows
 
     def body(
-        valid_hbm, recv_ref, keys_old, values_old, conv_kept, conv_part, taps_f32, weight_hbm,
+        valid_hbm, recv_ref, keys_old, values_old, conv_kept, conv_part, taps_f32, first_weight,
+        second_weight, weight_hbm,
         encoded_hbm, keys_next_hbm, values_next_hbm, conv_next_hbm,
         encoded_ref, keys_next_ref, values_next_ref, conv_next_ref,
         weight_ref, gathered, qkv_ref, attended_ref, attended_f32, encoded_f32, valid_ref,
         weight_sems, out_sems, valid_sem,
     ):
+        parts = [(2 * near if n == 0 else 0, a, b) for n, (a, b) in enumerate(zip(edges, edges[1:]))]
         weight_copies = [
             pltpu.make_async_copy(
-                weight_hbm.at[:, first:last], weight_ref.at[:, first:last], weight_sems.at[n]
+                weight_hbm.at[top:, first:last], weight_ref.at[top:, first:last], weight_sems.at[n]
             )
-            for n, (first, last) in enumerate(zip(edges, edges[1:]))
+            for n, (top, first, last) in enumerate(parts)
         ]
         for copy in weight_copies:
             copy.start()
@@ -403,9 +421,13 @@
         normed = (centered * lax.rsqrt(spread_of + EPSILON)).astype(BF16)
 
         def project(n):
+            top, first, last = parts[n]
             weight_copies[n].wait()
-            columns_of = slice(edges[n], edges[n + 1])
-            qkv_ref[:, columns_of] = matmul(normed, weight_ref[:, columns_of]).astype(BF16)
+            weight = weight_ref[top:, first:last]
+            if top:
+                near_weights = [ref[...].reshape(near, width) for ref in (first_weight, second_weight)]
+                weight = jnp.concatenate([*near_weights, weight], axis=0)
+            qkv_ref[:, first:last] = matmul(normed, weight).astype(BF16)
 
         for n in range(VALUES_FROM):
             project(n)
@@ -554,7 +576,7 @@
     return pl.pallas_call(
         body,
         out_shape=[jax.ShapeDtypeStruct(shape, BF16) for shape in out_shapes],
-        in_specs=whole(pl.ANY, *[pltpu.VMEM] * 6, pl.ANY),
+        in_specs=whole(pl.ANY, *[pltpu.VMEM] * 8, pl.ANY),
         out_specs=whole(*[pl.ANY] * 4),
         scratch_shapes=[
             *[pltpu.VMEM(shape, BF16) for shape in out_shapes],
@@ -600,7 +622,7 @@
     received = lax.all_to_all(packed, "streams", split_axis=0, concat_axis=0, tiled=True)
     settled = settle_streams(
         from_lower, from_upper, destination, valid_count, key_cache, value_cache,
-        conv_by_time, conv_kernel, row_count // streams,
+        conv_by_time, conv_kernel, qkv_weight, row_count // streams,
     )
     encoded, keys_next, values_next, conv_next = stream_step(
         received, valid_count, settled, qkv_weight, peers, row_count, capacity

time: 42.8 us -> 42.6 us (level)
  transfers between devices with their start and end apart: 3 -> 3, of which waited for: 1 -> 1; matrix products, arithmetic and copies ran while one was open for 0% -> 0% of each run, Pallas kernels for 6% -> 7%
where the time goes in v6:
time: 42.6 us; the launch traced here: 42.2 us
  waiting for transfers between devices  17.9 us (42%)
  starting transfers between devices  11.9 us (28%)
  Pallas kernels  11.8 us (28%)
  between operations  0.67 us (2%)
    ppermute x2, waiting for transfers between devices, from_behind(): lax.ppermute(block, axis, [((i - distance) % count, i) for i in range(cou...  17.9 us
    all_to_all x1, starting transfers between devices, local(): lax.all_to_all(packed, 'streams', split_axis=0, concat_axis=0, tiled=True)  7.43 us
    pallas_call x1, Pallas kernels, stream_step(): pl.pallas_call(body, out_shape=[jax.ShapeDtypeStruct(shape, BF16) for sha...  6.35 us
    ppermute x2, starting transfers between devices, from_behind(): lax.ppermute(block, axis, [((i - distance) % count, i) for i in range(cou...  4.49 us
    pallas_call x1, Pallas kernels, settle_streams(): pl.pallas_call(body, out_shape=(pltpu.VMEM(cache, BF16), pltpu.VMEM(cache...  2.81 us
    pallas_call x1, Pallas kernels, pack_all(): pl.pallas_call(body, out_shape=(pltpu.HBM(packed_shape, BF16), bundle, bu...  2.63 us
  transfers between devices with their start and end apart: 3, of which 1 were waited for; matrix products, arithmetic and copies ran while one was open for 0% of the time, Pallas kernels for 7%

profile of v6, /device:TPU:0, one launch (start us, length us, event | category | flops | bytes accessed | tf_op | source)
XLA Modules:
  0.0 42.2 jit_solution(2418253543015930034)
XLA Ops:
  0.6 2.6 %pack_all.1 = (bf16[2432,128]{1,0:T(8,128)(2,1)}, bf16[4,96,768]{2,1,0:T(8,128)(2,1)S(1)}, bf16[4,96,768]{2,1,0:T(8,128)(2,1)S(1)}) custom-call(s32[8]{0:T(128)} %dest_hbm.3, s32[1]{0:T(128)} %bitcast.own_hbm, s32[1,128]{1,0:T(1,128)} %bitcast.17, s32[1,128]{1,0:T(1,128)} %bitcast.18, bf16[8,32,768]{2,1,0:T(8,128)(2,1)} %key_hbm.3, ...), custom_call_target="tpu_custom_call" | custom-call | tf_op jit(solution)/shard_map/pack_all/pallas_call | solution.py:183
  3.3 7.4 %all-to-all-start = ((bf16[16,152,128]{2,1,0:T(8,128)(2,1)}), bf16[16,152,128]{2,1,0:T(8,128)(2,1)S(1)}, u32[]{:S(2)}, u32[]{:S(2)}) async-start(bf16[16,152,128]{2,1,0:T(8,128)(2,1)} %bitcast.16), calls=%async_computation | async-start | bytes 1245184 | tf_op jit(solution)/shard_map/all_to_all | solution.py:622
  10.7 0.4 collective-permute-start
  11.1 4.1 %collective-permute-start.1 = (bf16[4,96,768]{2,1,0:T(8,128)(2,1)S(1)}, bf16[4,96,768]{2,1,0:T(8,128)(2,1)S(1)}, u32[]{:S(2)}, u32[]{:S(2)}) collective-permute-start(bf16[4,96,768]{2,1,0:T(8,128)(2,1)S(1)} %get-tuple-element.20), channel_id=1, source_target_pairs={{1,0},{2,1},{3,2},{4,3},{5,4},{6,5},{7,6},{8,7},{9,8},{10,9},{11,1... | collective-permute-start | bytes 1769480 | tf_op jit(solution)/shard_map/ppermute | solution.py:603
  15.2 17.9 %collective-permute-done.lower_ref = bf16[4,96,768]{2,1,0:T(8,128)(2,1)S(1)} collective-permute-done((bf16[4,96,768]{2,1,0:T(8,128)(2,1)S(1)}, bf16[4,96,768]{2,1,0:T(8,128)(2,1)S(1)}, u32[]{:S(2)}, u32[]{:S(2)}) %collective-permute-start) | collective-permute-done | bytes 589856 | tf_op jit(solution)/shard_map/ppermute | solution.py:603
  33.1 0.0 collective-permute-done.1.upper_ref
  33.1 2.8 %settle_streams.1 = (bf16[8,32,768]{2,1,0:T(8,128)(2,1)S(1)}, bf16[8,32,768]{2,1,0:T(8,128)(2,1)S(1)}, bf16[248,768]{1,0:T(8,128)(2,1)S(1)}, f32[6,128,128]{2,1,...) custom-call(s32[8]{0:T(128)} %dest_hbm.3, ...), custom_call_target="tpu_custom_call", output_to_operand_aliasing={{5}: (3, {}), {6}: (4, {})} | custom-call | tf_op jit(solution)/shard_map/settle_streams/pallas_call | solution.py:322
  35.9 0.0 all-to-all-done
  35.9 6.3 %stream_step.1 = (bf16[128,768]{1,0:T(8,128)(2,1)}, bf16[256,768]{1,0:T(8,128)(2,1)}, bf16[256,768]{1,0:T(8,128)(2,1)}, bf16[248,768]{1,0:T(8,128)(2,1)}) custom-call(s32[8]{0:T(128)} %valid_hbm.3, bf16[2432,128]{1,0:T(8,128)(2,1)S(1)} %bitcast.13, bf16[8,32,768]{2,1,0:T(8,128)(2,1)S(1)} %get-tuple-element.21.keys_old, ...), custom_call_target="tpu_custom_call" | custom-call | tf_op jit(solution)/shard_map/stream_step/pallas_call | solution.py:576
Async XLA Ops:
  3.3 32.6 %all-to-all-start = ((bf16[16,152,128]{2,1,0:T(8,128)(2,1)}), bf16[16,152,128]{2,1,0:T(8,128)(2,1)S(1)}, u32[]{:S(2)}, u32[]{:S(2)}) async-start(bf16[16,152,128]{2,1,0:T(8,128)(2,1)} %bitcast.16), calls=%async_computation | async-start | bytes 1245184 | tf_op jit(solution)/shard_map/all_to_all | solution.py:622
  10.7 22.4 %collective-permute-start = (bf16[4,96,768]{2,1,0:T(8,128)(2,1)S(1)}, bf16[4,96,768]{2,1,0:T(8,128)(2,1)S(1)}, u32[]{:S(2)}, u32[]{:S(2)}) collective-permute-start(bf16[4,96,768]{2,1,0:T(8,128)(2,1)S(1)} %get-tuple-element.19), channel_id=1, source_target_pairs={{15,0},{0,1},{1,2},{2,3},{3,4},{4,5},{5,6},{6,7},{7,8},{8,9},{9,10... | collective-permute-start | bytes 1769480 | tf_op jit(solution)/shard_map/ppermute | solution.py:603
  11.1 22.0 %collective-permute-start.1 = (bf16[4,96,768]{2,1,0:T(8,128)(2,1)S(1)}, bf16[4,96,768]{2,1,0:T(8,128)(2,1)S(1)}, u32[]{:S(2)}, u32[]{:S(2)}) collective-permute-start(bf16[4,96,768]{2,1,0:T(8,128)(2,1)S(1)} %get-tuple-element.20), channel_id=1, source_target_pairs={{1,0},{2,1},{3,2},{4,3},{5,4},{6,5},{7,6},{8,7},{9,8},{10,9},{11,1... | collective-permute-start | bytes 1769480 | tf_op jit(solution)/shard_map/ppermute | solution.py:603
